TPU v7x, 768 devices: a whole 4x8x12 slice. The times are simulated.
768 devices in a mesh: slab: 192 (over z, y_lo, x, core), col: 4 (over y_hi).
Axes of the slice: x: 4, y: 8 (y_hi: 4, y_lo: 2; y = y_hi * 2 + y_lo), z: 12, core: 2. Of those that a mesh axis runs over, the one named last changes fastest.
Arguments:
- density: float32 [384, 128, 256], P('slab', 'col'), may hold values from 0.5 to 2
- velocity: float32 [3, 384, 128, 256], P(None, 'slab', 'col'), may hold values from -3 to 3
- pressure: float32 [384, 128, 256], P('slab', 'col'), may hold values from 0.5 to 2
- fraction_code: int32 [384, 128, 256], P('slab', 'col'), may hold values from 8 to 16
- interface_cell: int32 [192, 4, 512], P('slab', 'col'), may hold values from 0 to 16383
- interface_element: int32 [192, 4, 512], P('slab', 'col'), may hold values from 0 to 511
- interface_count: int32 [192, 4], P('slab', 'col'), may hold values from 64 to 512, as said below
- wall_normal: float32 [3, 192, 4, 512], P(None, 'slab', 'col'), may hold values from -4 to 4
- element_mass: float32 [192, 512], P('slab'), may hold values from 0.5 to 2
- element_removed: int32 [192, 512], P('slab'), may hold values 0 or 1
- element_velocity: float32 [3, 192, 512], P(None, 'slab'), may hold values from -3 to 3
Outputs:
- new_state: float32 [5, 384, 128, 256], P(None, 'slab', 'col')
- new_velocity: float32 [3, 192, 512], P(None, 'slab', 'col')
Inputs may be any that keep to these rules, and one draw needn't show every extreme that they name: `interface_cell`: index within the block of 2 x 32 x 256 cells of its slab and column. `interface_element`: element of the row's own slab group. `interface_count`: each count is 512, 256, 128 or 64; some slab and column has 512.
All inputs are finite; a program needn't handle non-finite values. No bound on the sum of `element_removed` on one device may be relied on, other than what follows from the above.
Results may differ from a plain program's by a relative error of at most 0.0003.
Values sent between devices are 32-bit elements; how exact they have to be, the bound alone decides.
No kernel may reach another device: no remote copies, remote signals or barrier semaphores. Data moves between devices by JAX's collectives and lax.ppermute only.
A program may use at most 64 MiB of HBM per device.

v0:
```python
import jax
import jax.numpy as jnp
from jax import lax
from jax.sharding import PartitionSpec as P

ratio_heat = 1.4
step_ratio = 0.1
struct_step = 1.0


def with_halo(array, sides, width):
    for axis, dim in sides:
        count, length = (lax.axis_size(axis), array.shape[dim])
        up = [(i, (i + 1) % count) for i in range(count - 1)]
        down = [(j, i) for i, j in up]
        last = lax.slice_in_dim(array, length - width, length, axis=dim)
        first = lax.slice_in_dim(array, 0, width, axis=dim)
        before = lax.ppermute(last, axis, up)
        after = lax.ppermute(first, axis, down)
        array = jnp.concatenate([before, array, after], axis=dim)
    return array


def cell_terms(density_s, velocity_s, pressure_s, along):
    normal = velocity_s[along]
    energy = pressure_s / (ratio_heat - 1.0) + 0.5 * density_s * (
        velocity_s[0] * velocity_s[0]
        + velocity_s[1] * velocity_s[1]
        + velocity_s[2] * velocity_s[2]
    )
    conserved = jnp.stack(
        [
            density_s,
            density_s * velocity_s[0],
            density_s * velocity_s[1],
            density_s * velocity_s[2],
            energy,
        ]
    )
    zero_plane = jnp.zeros_like(pressure_s)
    pressure_terms = [zero_plane, zero_plane, zero_plane, zero_plane, pressure_s * normal]
    pressure_terms[1 + along] = pressure_s
    flux_terms = normal[None] * conserved + jnp.stack(pressure_terms)
    wave_speed = jnp.abs(normal) + jnp.sqrt(ratio_heat * pressure_s / density_s)
    return (conserved, flux_terms, wave_speed)


def cut_range(array, start, stop, along):
    return lax.slice_in_dim(array, start, stop, axis=array.ndim - 3 + along)


def face_sum(conserved, flux_terms, wave_speed, fraction, along):
    extent = fraction.shape[along]

    def take_low(array):
        return cut_range(array, 0, extent - 1, along)

    def take_high(array):
        return cut_range(array, 1, extent, along)

    face_flux = 0.5 * (take_low(flux_terms) + take_high(flux_terms)) - 0.5 * jnp.maximum(
        take_low(wave_speed), take_high(wave_speed)
    )[None] * (take_high(conserved) - take_low(conserved))
    weighted = jnp.minimum(take_low(fraction), take_high(fraction))[None] * face_flux
    return cut_range(weighted, 1, extent - 1, along) - cut_range(weighted, 0, extent - 2, along)


def interior(array, along):
    for other in range(3):
        if other != along:
            array = cut_range(array, 1, array.shape[array.ndim - 3 + other] - 1, other)
    return array


def divergence(density_p, velocity_p, pressure_p, fraction_p):
    live = fraction_p > 0.0
    density_s = jnp.where(live, density_p, 1.0)
    pressure_s = jnp.where(live, pressure_p, 1.0)
    summed = 0.0
    for along in range(3):
        conserved, flux_terms, wave_speed = cell_terms(
            interior(density_s, along),
            interior(velocity_p, along),
            interior(pressure_s, along),
            along,
        )
        summed = summed + face_sum(
            conserved, flux_terms, wave_speed, interior(fraction_p, along), along
        )
    return summed


def local(
    density,
    velocity,
    pressure,
    fraction_code,
    interface_cell,
    interface_element,
    interface_count,
    wall_normal,
    element_mass,
    element_removed,
    element_velocity,
):
    block_x, block_y, block_z = density.shape
    block_cells = block_x * block_y * block_z
    fraction = fraction_code.astype(jnp.float32) / 16.0
    cell_ids = interface_cell.reshape(-1)
    elem_ids = interface_element.reshape(-1)
    row_total = cell_ids.shape[0]
    normals = wall_normal.reshape(3, row_total)
    row_pressure = pressure.reshape(-1)[cell_ids]
    row_fraction = fraction.reshape(-1)[cell_ids]
    active = (jnp.arange(row_total, dtype=jnp.int32) < interface_count.reshape(())).astype(
        jnp.float32
    )
    weight = row_pressure * (1.0 - row_fraction) * active
    wall_force = -weight[None] * normals
    group_size = element_mass.shape[1]
    onehot = (elem_ids[:, None] == jnp.arange(group_size, dtype=jnp.int32)[None, :]).astype(
        jnp.float32
    )
    partial_value = jnp.dot(wall_force, onehot, precision=lax.Precision.HIGHEST)
    all_mass = element_mass.reshape(group_size)
    keep_factor = 1.0 - element_removed.reshape(group_size).astype(jnp.float32)
    start_motion = element_velocity.reshape(3, group_size)
    own_share = group_size // lax.axis_size("col")
    own_start = lax.axis_index("col") * own_share
    elem_loads = lax.psum_scatter(partial_value, "col", scatter_dimension=1, tiled=True)
    own_mass = lax.dynamic_slice_in_dim(all_mass, own_start, own_share)
    own_keep = lax.dynamic_slice_in_dim(keep_factor, own_start, own_share)
    own_motion = lax.dynamic_slice_in_dim(start_motion, own_start, own_share, 1)
    new_motion = (own_motion + struct_step * elem_loads / own_mass[None]) * own_keep[None]
    wall_motion = lax.all_gather(new_motion, "col", axis=1, tiled=True)
    row_motion = jnp.dot(wall_motion, onehot.T, precision=lax.Precision.HIGHEST)
    wall_work = weight * jnp.sum(normals * row_motion, axis=0)
    row_terms = jnp.concatenate([weight[None] * normals, wall_work[None]], axis=0)
    source = jnp.zeros((4, block_cells), jnp.float32).at[:, cell_ids].add(row_terms)
    source = jnp.concatenate([jnp.zeros((1, block_cells), jnp.float32), source], axis=0).reshape(
        5, block_x, block_y, block_z
    )
    centre = cell_terms(density, velocity, pressure, 0)[0]
    z_pad = ((0, 0), (0, 0), (0, 0), (1, 1))
    stacked = jnp.concatenate([density[None], velocity, pressure[None], fraction[None]], axis=0)
    widened = with_halo(stacked, (("slab", 1), ("col", 2)), 1)
    widened = jnp.pad(widened, z_pad)
    summed = divergence(widened[0], widened[1:4], widened[4], widened[5])
    new_state = centre - step_ratio / fraction[None] * (summed - source)
    return (new_state, new_motion.reshape(3, 1, own_share))


def solution(mesh):
    placed = (
        P("slab", "col", None),
        P(None, "slab", "col", None),
        P("slab", "col", None),
        P("slab", "col", None),
        P("slab", "col", None),
        P("slab", "col", None),
        P("slab", "col"),
        P(None, "slab", "col", None),
        P("slab", None),
        P("slab", None),
        P(None, "slab", None),
    )
    return jax.shard_map(
        local,
        mesh=mesh,
        in_specs=placed,
        out_specs=(P(None, "slab", "col", None), P(None, "slab", "col")),
        check_vma=False,
    )
```

profile of v0, /device:TPU:16, one launch (start us, length us, event | category | flops | bytes accessed | tf_op | source)
XLA Modules:
  0.0 109.0 jit_solution(15970003930344796096)
XLA Ops:
  7.2 0.7 compare_select_fusion
  8.6 0.9 copy.26
  9.5 0.9 broadcast_divide_fusion
  10.4 3.1 %gather_fusion = f32[512]{0:T(512)S(1)} fusion(f32[16384]{0:T(1024)S(1)} %bitcast.189, s32[1024]{0:T(1024)S(1)} %pad_clamp_fusion), kind=kCustom, calls=%fused_computation | custom fusion | bytes 6144 | tf_op jit(solution)/shard_map/gather | solution.py:113
  13.6 3.1 %gather_fusion.1 = f32[512]{0:T(512)S(1)} fusion(f32[16384]{0:T(1024)S(1)} %bitcast.190, s32[1024]{0:T(1024)S(1)} %pad_clamp_fusion), kind=kCustom, calls=%fused_computation.1 | custom fusion | bytes 6144 | tf_op jit(solution)/shard_map/gather | solution.py:114
  16.8 1.8 %convolution_bitcast_fusion = f32[512,3]{1,0:T(8,128)} fusion(s32[512]{0:T(512)S(1)} %bitcast.212, f32[3,1,1,512]{3,2,1,0:T(1,128)S(1)} %copy-done.4, f32[512]{0:T(512)S(1)} %get-tuple-element.16), kind=kOutput, calls=%fused_computation.12 | convolution fusion | flops 9700864 | bytes 16384
  18.7 1.3 %collective-permute-start.1 = (f32[6,1,32,256]{3,2,1,0:T(8,128)S(1)}, f32[6,1,32,256]{3,2,1,0:T(8,128)S(1)}, u32[]{:S(2)}, u32[]{:S(2)}) collective-permute-start(f32[6,1,32,256]{3,2,1,0:T(8,128)S(1)} %get-tuple-element.30), channel_id=1, source_target_pairs={{4,0},{8,4},{12,8},{16,12},{20,16},{24,20},{28,24},{32,28},{36,32}... | collective-permute-start | bytes 589832 | tf_op jit(solution)/shard_map/ppermute | solution.py:19
  20.0 3.0 %collective-permute-start = (f32[6,1,32,256]{3,2,1,0:T(8,128)S(1)}, f32[6,1,32,256]{3,2,1,0:T(8,128)S(1)}, u32[]{:S(2)}, u32[]{:S(2)}) collective-permute-start(f32[6,1,32,256]{3,2,1,0:T(8,128)S(1)} %get-tuple-element.29), channel_id=1, source_target_pairs={{0,4},{4,8},{8,12},{12,16},{16,20},{20,24},{24,28},{28,32},{32,36}... | collective-permute-start | bytes 589832 | tf_op jit(solution)/shard_map/ppermute | solution.py:18
  23.3 0.7 fusion.43
  24.0 32.4 %reduce-scatter.4.cloned.1.call-done = f32[128,3]{1,0:T(8,128)} async-done(((f32[512,3]{1,0:T(8,128)}), f32[128,3]{1,0:T(8,128)}) %reduce-scatter.4.cloned.1.call-update) | async-done | bytes 1552
  56.4 0.9 copy.23
  57.3 12.5 %all_gather.3 = f32[3,512]{1,0:T(4,128)S(1)} all-gather(f32[3,128]{1,0:T(4,128)S(1)} %fusion.41), channel_id=1, replica_groups=mesh['slab'=192,'col'=4] {'col'}, dimensions={1}, use_global_device_ids=true | all-gather | bytes 7680 | tf_op jit(solution)/shard_map/all_gather | solution.py:135
  69.8 0.7 fusion.2
  70.6 2.4 %collective-permute-start.3 = (f32[6,4,1,256]{3,2,1,0:T(1,128)S(1)}, f32[6,4,1,256]{3,2,1,0:T(1,128)S(1)}, u32[]{:S(2)}, u32[]{:S(2)}) collective-permute-start(f32[6,4,1,256]{3,2,1,0:T(1,128)S(1)} %get-tuple-element.28), channel_id=1, source_target_pairs={{1,0},{2,1},{3,2},{5,4},{6,5},{7,6},{9,8},{10,9},{11,10},{13,12},{... | collective-permute-start | bytes 73736 | tf_op jit(solution)/shard_map/ppermute | solution.py:19
  73.0 5.5 %collective-permute-start.2 = (f32[6,4,1,256]{3,2,1,0:T(1,128)S(1)}, f32[6,4,1,256]{3,2,1,0:T(1,128)S(1)}, u32[]{:S(2)}, u32[]{:S(2)}) collective-permute-start(f32[6,4,1,256]{3,2,1,0:T(1,128)S(1)} %get-tuple-element.27), channel_id=1, source_target_pairs={{0,1},{1,2},{2,3},{4,5},{5,6},{6,7},{8,9},{9,10},{10,11},{12,13},{... | collective-permute-start | bytes 73736 | tf_op jit(solution)/shard_map/ppermute | solution.py:18
  78.5 0.1 copy.19
  78.7 6.0 %scatter_custom_fusion = f32[4,16384]{0,1:T(8,128)} fusion(s32[512]{0:T(512)S(1)} %bitcast.209, f32[512,4]{1,0:T(8,128)S(1)} %copy.19, f32[]{:T(128)} %constant.16.clone.1), kind=kCustom, calls=%fused_computation.3 | custom fusion | flops 2048 | bytes 262148 | tf_op jit(solution)/shard_map/scatter-add | solution.py:139
  84.7 6.6 %concatenate.19 = f32[5,16384]{0,1:T(8,128)} pad(f32[4,16384]{0,1:T(8,128)} %scatter_custom_fusion, f32[]{:T(128)} %constant.16.clone.1), padding=1_0x0_0 | pad | bytes 589828 | tf_op jit(solution)/shard_map/concatenate | solution.py:140
  91.3 5.3 %copy.20 = f32[5,2,32,256]{3,2,1,0:T(8,128)S(1)} copy(f32[5,2,32,256]{0,3,2,1:T(8,128)} %bitcast.191) | data formatting | bytes 655360 | tf_op jit(solution)/shard_map/reshape | solution.py:140
  96.5 0.6 copy.21
  97.1 0.1 pad_maximum_fusion
  97.2 0.2 fusion.26
  97.5 0.1 fusion.24
  97.9 0.1 sqrt_add_fusion.2
  98.6 0.1 bitcast_dynamic-update-slice_fusion.5
  99.4 0.2 sqrt_add_fusion
  100.0 0.3 fusion.7
  100.5 0.1 fusion.15
  100.8 0.1 bitcast_dynamic-update-slice_fusion
  101.0 0.2 maximum_add_fusion
  101.1 0.1 fusion.11
  101.3 0.9 fusion.20
  (60 shorter events, 2.7 us)
Async XLA Ops:
  7.2 16.0 %copy-start = (f32[3,1,512]{2,1,0:T(1,128)S(1)}, f32[3,1,512]{2,1,0:T(1,128)}, u32[]{:S(2)}) copy-start(f32[3,1,512]{2,1,0:T(1,128)} %param.21) | copy-start | bytes 18436
  7.2 49.2 %reduce-scatter.4.cloned.1.call-start = ((), (), s32[]{:S(2)}) async-start(), calls=%async_computation.1 | async-start | bytes 327680
  13.5 3.2 %copy-start.4 = (f32[3,1,1,512]{3,2,1,0:T(1,128)S(1)}, f32[3,1,1,512]{3,2,1,0:T(1,128)}, u32[]{:S(2)}) copy-start(f32[3,1,1,512]{3,2,1,0:T(1,128)} %param.18) | copy-start | bytes 18436
  13.5 3.2 %copy-start.5 = (s32[1,1,512]{2,1,0:T(1,128)S(1)}, s32[1,1,512]{2,1,0:T(1,128)}, u32[]{:S(2)}) copy-start(s32[1,1,512]{2,1,0:T(1,128)} %param.16) | copy-start | bytes 6148
  13.5 5.0 %copy-start.1 = (f32[3,2,32,256]{3,2,1,0:T(8,128)S(1)}, f32[3,2,32,256]{3,2,1,0:T(8,128)}, u32[]{:S(2)}) copy-start(f32[3,2,32,256]{3,2,1,0:T(8,128)} %param.12) | copy-start | bytes 589828
  13.5 5.0 %copy-start.2 = (f32[2,32,256]{2,1,0:T(8,128)S(1)}, f32[2,32,256]{2,1,0:T(8,128)}, u32[]{:S(2)}) copy-start(f32[2,32,256]{2,1,0:T(8,128)} %param.11) | copy-start | bytes 196612
  13.6 5.0 %copy-start.3 = (f32[2,32,256]{2,1,0:T(8,128)S(1)}, f32[2,32,256]{2,1,0:T(8,128)}, u32[]{:S(2)}) copy-start(f32[2,32,256]{2,1,0:T(8,128)} %param.13) | copy-start | bytes 196612
  18.7 51.8 %collective-permute-start.1 = (f32[6,1,32,256]{3,2,1,0:T(8,128)S(1)}, f32[6,1,32,256]{3,2,1,0:T(8,128)S(1)}, u32[]{:S(2)}, u32[]{:S(2)}) collective-permute-start(f32[6,1,32,256]{3,2,1,0:T(8,128)S(1)} %get-tuple-element.30), channel_id=1, source_target_pairs={{4,0},{8,4},{12,8},{16,12},{20,16},{24,20},{28,24},{32,28},{36,32}... | collective-permute-start | bytes 589832 | tf_op jit(solution)/shard_map/ppermute | solution.py:19
  20.0 50.5 %collective-permute-start = (f32[6,1,32,256]{3,2,1,0:T(8,128)S(1)}, f32[6,1,32,256]{3,2,1,0:T(8,128)S(1)}, u32[]{:S(2)}, u32[]{:S(2)}) collective-permute-start(f32[6,1,32,256]{3,2,1,0:T(8,128)S(1)} %get-tuple-element.29), channel_id=1, source_target_pairs={{0,4},{4,8},{8,12},{12,16},{16,20},{20,24},{24,28},{28,32},{32,36}... | collective-permute-start | bytes 589832 | tf_op jit(solution)/shard_map/ppermute | solution.py:18
  70.6 26.5 %collective-permute-start.3 = (f32[6,4,1,256]{3,2,1,0:T(1,128)S(1)}, f32[6,4,1,256]{3,2,1,0:T(1,128)S(1)}, u32[]{:S(2)}, u32[]{:S(2)}) collective-permute-start(f32[6,4,1,256]{3,2,1,0:T(1,128)S(1)} %get-tuple-element.28), channel_id=1, source_target_pairs={{1,0},{2,1},{3,2},{5,4},{6,5},{7,6},{9,8},{10,9},{11,10},{13,12},{... | collective-permute-start | bytes 73736 | tf_op jit(solution)/shard_map/ppermute | solution.py:19
  73.0 24.1 %collective-permute-start.2 = (f32[6,4,1,256]{3,2,1,0:T(1,128)S(1)}, f32[6,4,1,256]{3,2,1,0:T(1,128)S(1)}, u32[]{:S(2)}, u32[]{:S(2)}) collective-permute-start(f32[6,4,1,256]{3,2,1,0:T(1,128)S(1)} %get-tuple-element.27), channel_id=1, source_target_pairs={{0,1},{1,2},{2,3},{4,5},{5,6},{6,7},{8,9},{9,10},{10,11},{12,13},{... | collective-permute-start | bytes 73736 | tf_op jit(solution)/shard_map/ppermute | solution.py:18
Sparse Core Ops, SparseCore 0:
  18.7 37.6 reduce-scatter.3
where the time goes:
time: 109 us
  waiting for transfers between devices  32.4 us (30%)
  local copies, waits for them, and re-layouts  21.2 us (19%)
  between operations  15.2 us (14%)
  other arithmetic  12.9 us (12%)
  blocking collectives  12.5 us (11%)
  starting transfers between devices  12.3 us (11%)
  matrix products  2.45 us (2%)
    unnamed x2, waiting for transfers between devices  32.4 us
    all_gather x1, blocking collectives, local(): wall_motion = lax.all_gather(new_motion, 'col', axis=1, tiled=True)  12.5 us
    ppermute x2, starting transfers between devices, with_halo(): before = lax.ppermute(last, axis, up)  8.55 us
    concatenate x1, local copies, waits for them, and re-layouts, local(): jnp.concatenate([jnp.zeros((1, block_cells), jnp.float32), source], axis=0)  6.56 us
    scatter-add x1, other arithmetic, local(): jnp.zeros((4, block_cells), jnp.float32).at[:, cell_ids].add(row_terms)  6 us
    reshape x1, local copies, waits for them, and re-layouts, local(): jnp.concatenate([jnp.zeros((1, block_cells), jnp.float32), source], axis=0)  5.26 us
    ppermute x2, starting transfers between devices, with_halo(): after = lax.ppermute(first, axis, down)  3.74 us
    gather x1, local copies, waits for them, and re-layouts, local(): row_pressure = pressure.reshape(-1)[cell_ids]  3.14 us
  transfers between devices with their start and end apart: 5, of which 1 were waited for; matrix products, arithmetic and copies ran while one was open for 19% of the time, Pallas kernels for 0%

commit v1 on v0

v1 whole, which is shorter than its diff:
```python
import jax
import jax.numpy as jnp
from jax import lax
from jax.experimental import pallas as pl
from jax.experimental.pallas import tpu as pltpu
from jax.sharding import PartitionSpec as P

ratio_heat = 1.4
step_ratio = 0.1
struct_step = 1.0

F32, BF16, I32 = jnp.float32, jnp.bfloat16, jnp.int32
TILE = 8
LOADS_AT = 16


def split3(value):
    high = value.astype(BF16).astype(F32)
    rest = value - high
    middle = rest.astype(BF16).astype(F32)
    return high, middle, rest - middle


def stack_rows(rows, total):
    index = lax.broadcasted_iota(I32, (total, rows[0].shape[1]), 0)
    out = jnp.zeros((total, rows[0].shape[1]), F32)
    for at, row in enumerate(rows):
        out = jnp.where(index == at, row, out)
    return out


def gather_kernel(count_in, cell_in, element_in, *refs):
    given, kept = refs[:8], refs[8:16]
    near_ref, far_ref, message, weight_ref, third_hot, plane_hot, element_hot = refs[16:23]
    count, cell, element, sems = refs[23:]
    density, velocity, pressure, code, normal = kept[:5]
    pairs = [(cell_in, cell), (element_in, element), (count_in, count)] + list(zip(given, kept))
    copies = [pltpu.make_async_copy(a, b, sems.at[i]) for i, (a, b) in enumerate(pairs)]
    for copy in copies:
        copy.start()
    for copy in copies:
        copy.wait()
    block_x, block_y, block_z = density.shape
    rows = cell.shape[2]
    group = element_hot.shape[0]
    odd = lax.rem(lax.axis_index("slab"), 2)
    col = lax.axis_index("col")

    for target, at in ((near_ref, 1 - odd), (far_ref, odd)):
        target[0] = density[at]
        for k in range(3):
            target[1 + k] = velocity[k, at]
        target[4] = pressure[at]
        target[5] = code[at].astype(F32) * (1.0 / 16.0)

    def edge(x, y):
        out = [density[x, y : y + 1]]
        out += [velocity[k, x, y : y + 1] for k in range(3)]
        out += [pressure[x, y : y + 1], code[x, y : y + 1].astype(F32) * (1.0 / 16.0)]
        return out

    for x in range(block_x):
        first, last = edge(x, 0), edge(x, block_y - 1)
        for j in range(message.shape[0]):
            for f in range(6):
                at = f * block_x + x
                message[j, at : at + 1] = jnp.where(col < j, last[f], first[f])

    fraction = code[...].astype(F32) * (1.0 / 16.0)
    table = (pressure[...] * (1.0 - fraction)).reshape(block_x * block_y, block_z)
    place = cell[0]
    third = jnp.bitwise_and(place, block_z - 1)
    plane = lax.shift_right_logical(place, block_z.bit_length() - 1)
    third_mask = lax.broadcasted_iota(I32, (block_z, rows), 0) == third
    third_hot[...] = jnp.where(third_mask, 1.0, 0.0).astype(BF16)
    plane_mask = lax.broadcasted_iota(I32, (block_x * block_y, rows), 0) == plane
    plane_hot[...] = jnp.where(plane_mask, 1.0, 0.0).astype(BF16)
    element_mask = lax.broadcasted_iota(I32, (group, rows), 0) == element[0]
    element_hot[...] = jnp.where(element_mask, 1.0, 0.0).astype(BF16)
    parts = jnp.concatenate(split3(table), axis=0).astype(BF16)
    found = jnp.dot(parts, third_hot[...], preferred_element_type=F32)
    n = block_x * block_y
    found = found[:n] + found[n : 2 * n] + found[2 * n :]
    found = jnp.sum(jnp.where(plane_mask, found, 0.0), axis=0, keepdims=True)
    live = lax.broadcasted_iota(I32, (1, rows), 1) < count[...]
    weight = jnp.where(live, found, 0.0)
    weight_ref[...] = weight

    split = [split3(-weight * normal[k, 0]) for k in range(3)]
    force = stack_rows([split[k][i] for i in range(3) for k in range(3)], 16).astype(BF16)
    partial = lax.dot_general(
        force, element_hot[...], (((1,), (1,)), ((), ())), preferred_element_type=F32
    )
    half = group // 2
    for k in range(3):
        total = partial[k : k + 1] + partial[3 + k : 4 + k] + partial[6 + k : 7 + k]
        for h in range(2):
            at = LOADS_AT + 2 * k + h
            for j in range(message.shape[0]):
                message[j, at : at + 1] = total[:, h * half : (h + 1) * half]


def derive(density, v0, v1, v2, pressure):
    m0, m1, m2 = density * v0, density * v1, density * v2
    energy = pressure * (1.0 / 0.4) + 0.5 * density * (v0 * v0 + v1 * v1 + v2 * v2)
    sound = jnp.sqrt(ratio_heat * pressure / density)
    return m0, m1, m2, energy, sound


RHO, V0, V1, V2, PRS, FRAC, M0, M1, M2, ENE, SND = range(11)


def face(along, low, high):
    vl, vh = low[V0 + along], high[V0 + along]
    speed = jnp.maximum(jnp.abs(vl) + low[SND], jnp.abs(vh) + high[SND])
    half = 0.5 * jnp.minimum(low[FRAC], high[FRAC])
    out = []
    for i, name in enumerate((RHO, M0, M1, M2, ENE)):
        if name == RHO:
            both = low[M0 + along] + high[M0 + along]
        elif name == ENE:
            both = vl * (low[ENE] + low[PRS]) + vh * (high[ENE] + high[PRS])
        else:
            both = vl * low[name] + vh * high[name]
            if i == 1 + along:
                both = both + (low[PRS] + high[PRS])
        out.append(half * (both - speed * (high[name] - low[name])))
    return out


def step_kernel(
    density,
    velocity,
    pressure,
    code,
    normal,
    mass,
    removed,
    motion,
    near_ref,
    far_ref,
    message,
    weight_ref,
    third_hot,
    plane_hot,
    element_hot,
    state_out,
    motion_out,
    cells,
    source,
    state,
    own_motion,
    state_sem,
    motion_sem,
):
    block_x, block_y, block_z = density.shape
    group = mass.shape[1]
    share = motion_out.shape[2]
    cols = message.shape[0]
    odd = lax.rem(lax.axis_index("slab"), 2)
    col = lax.axis_index("col")
    half = group // 2
    pad = TILE

    keep = 1.0 - removed[...].astype(F32)
    new = []
    for k in range(3):
        at = LOADS_AT + 2 * k
        load = message[0, at : at + 2]
        for j in range(1, cols):
            load = load + message[j, at : at + 2]
        load = jnp.concatenate([load[0:1], load[1:2]], axis=1)
        new.append((motion[k] + struct_step * load / mass[...]) * keep)
        own = new[k][:, 0:share]
        for j in range(1, cols):
            own = jnp.where(col == j, new[k][:, j * share : (j + 1) * share], own)
        own_motion[k] = own
    motion_copy = pltpu.make_async_copy(own_motion, motion_out, motion_sem)
    motion_copy.start()
    split = [split3(value) for value in new]
    stacked = stack_rows([split[k][i] for i in range(3) for k in range(3)], 16).astype(BF16)
    moved = jnp.dot(stacked, element_hot[...], preferred_element_type=F32)
    weight = weight_ref[...]
    work = jnp.zeros_like(weight)
    values = []
    for k in range(3):
        row = moved[k : k + 1] + moved[3 + k : 4 + k] + moved[6 + k : 7 + k]
        work = work + normal[k, 0] * row
        values.append(weight * normal[k, 0])
    values.append(weight * work)
    hot = plane_hot[...]
    parts = [split3(value) for value in values]
    for k in range(4):
        left = jnp.concatenate([hot * parts[k][i].astype(BF16) for i in range(3)], axis=0)
        found = lax.dot_general(
            left, third_hot[...], (((1,), (1,)), ((), ())), preferred_element_type=F32
        )
        n = block_x * block_y
        source[k] = (found[:n] + found[n : 2 * n] + found[2 * n :]).reshape(
            block_x, block_y, block_z
        )

    def store(plane, at, count, prims, fraction):
        full = list(prims) + [fraction] + list(derive(*prims))
        for name, value in enumerate(full):
            cells[name, plane, at : at + count] = value

    for x in range(block_x):
        for t in range(block_y // TILE):
            at = slice(t * TILE, (t + 1) * TILE)
            prims = [density[x, at]] + [velocity[k, x, at] for k in range(3)] + [pressure[x, at]]
            store(1 + x, pad + t * TILE, TILE, prims, code[x, at].astype(F32) * (1.0 / 16.0))
    for ref, plane in ((near_ref, 3 * (1 - odd)), (far_ref, 3 * odd)):
        for t in range(block_y // TILE):
            at = slice(t * TILE, (t + 1) * TILE)
            fraction = ref[5, at]
            live = fraction > 0.0
            prims = [jnp.where(live, ref[0, at], 1.0)] + [ref[1 + k, at] for k in range(3)]
            prims.append(jnp.where(live, ref[4, at], 1.0))
            store(plane, pad + t * TILE, TILE, prims, fraction)
    for other, inside, at in (
        (jnp.maximum(col - 1, 0), col > 0, pad - 1),
        (jnp.minimum(col + 1, cols - 1), col < cols - 1, pad + block_y),
    ):
        for x in range(block_x):
            prims = [message[other, f * block_x + x][None] for f in range(5)]
            fraction = message[other, 5 * block_x + x][None]
            store(1 + x, at, 1, prims, jnp.where(inside, fraction, 0.0))

    lane = lax.broadcasted_iota(I32, (TILE, block_z), 1)
    row = lax.broadcasted_iota(I32, (TILE, block_z), 0)

    def load(plane, at, along):
        out = {}
        for name in (RHO, V0 + along, PRS, FRAC, M0, M1, M2, ENE, SND):
            out[name] = cells[name, plane, at : at + TILE]
        return out

    for x in range(block_x):
        before = None
        for t in range(-1, block_y // TILE):
            at = pad + t * TILE
            upper = face(1, load(1 + x, at, 1), load(1 + x, at + 1, 1))
            turned = [pltpu.roll(value, 1, 0) for value in upper]
            if t < 0:
                before = turned
                continue
            total = [
                value - jnp.where(row == 0, old, fresh)
                for value, old, fresh in zip(upper, before, turned)
            ]
            before = turned
            own = load(1 + x, at, 2)
            right = {name: pltpu.roll(value, block_z - 1, 1) for name, value in own.items()}
            right[FRAC] = jnp.where(lane == block_z - 1, 0.0, right[FRAC])
            upper = face(2, own, right)
            total = [
                value + (flux - pltpu.roll(flux, 1, 1)) for value, flux in zip(total, upper)
            ]
            own = load(1 + x, at, 0)
            upper = face(0, own, load(2 + x, at, 0))
            lower = face(0, load(x, at, 0), own)
            total = [value + (u - v) for value, u, v in zip(total, upper, lower)]
            scale = step_ratio / own[FRAC]
            rows = slice(t * TILE, (t + 1) * TILE)
            for i, name in enumerate((RHO, M0, M1, M2, ENE)):
                change = total[i] - source[i - 1, x, rows] if i else total[i]
                state[i, x, rows] = own[name] - scale * change
        pltpu.make_async_copy(state.at[:, x], state_out.at[:, x], state_sem.at[x]).start()
    for x in range(block_x):
        pltpu.make_async_copy(state.at[:, x], state_out.at[:, x], state_sem.at[x]).wait()
    motion_copy.wait()


def in_vmem(*arrays):
    return [pltpu.with_memory_space_constraint(array, pltpu.VMEM) for array in arrays]


def local(
    density,
    velocity,
    pressure,
    fraction_code,
    interface_cell,
    interface_element,
    interface_count,
    wall_normal,
    element_mass,
    element_removed,
    element_velocity,
):
    block_x, block_y, block_z = density.shape
    rows = interface_cell.shape[2]
    group = element_mass.shape[1]
    slabs, cols = lax.axis_size("slab"), lax.axis_size("col")
    share = group // cols
    vmem = pl.BlockSpec(memory_space=pltpu.VMEM)
    hbm = pl.BlockSpec(memory_space=pltpu.HBM)
    given = (
        density,
        velocity,
        pressure,
        fraction_code,
        wall_normal,
        element_mass,
        element_removed,
        element_velocity,
    )
    results = pl.pallas_call(
        gather_kernel,
        out_shape=tuple(pltpu.VMEM(array.shape, array.dtype) for array in given)
        + (
            pltpu.VMEM((6, block_y, block_z), F32),
            pltpu.VMEM((6, block_y, block_z), F32),
            pltpu.VMEM((cols, 24, block_z), F32),
            pltpu.VMEM((1, rows), F32),
            pltpu.VMEM((block_z, rows), BF16),
            pltpu.VMEM((block_x * block_y, rows), BF16),
            pltpu.VMEM((group, rows), BF16),
        ),
        in_specs=[pl.BlockSpec(memory_space=pl.ANY)] + [hbm] * 10,
        out_specs=[vmem] * 15,
        scratch_shapes=[
            pltpu.VMEM(interface_count.shape, I32),
            pltpu.VMEM(interface_cell.shape, I32),
            pltpu.VMEM(interface_element.shape, I32),
            pltpu.SemaphoreType.DMA((11,)),
        ],
        name="gather_rows",
    )(
        interface_count,
        interface_cell,
        interface_element,
        *given,
    )
    kept, (near, far, message), hots = results[:8], results[8:11], results[11:]

    inner = [(i, i ^ 1) for i in range(slabs)]
    outer = [(i, i + 1 if i % 2 else i - 1) for i in range(1, slabs - 1)]
    near_in = lax.ppermute(near, "slab", inner)
    far_in = lax.ppermute(far, "slab", outer)
    message_in = lax.all_to_all(message, "col", 0, 0)

    state, new_motion = pl.pallas_call(
        step_kernel,
        out_shape=(
            jax.ShapeDtypeStruct((5, block_x, block_y, block_z), F32),
            jax.ShapeDtypeStruct((3, 1, share), F32),
        ),
        in_specs=[vmem] * 15,
        out_specs=[hbm, hbm],
        scratch_shapes=[
            pltpu.VMEM((11, block_x + 2, block_y + 2 * TILE, block_z), F32),
            pltpu.VMEM((4, block_x, block_y, block_z), F32),
            pltpu.VMEM((5, block_x, block_y, block_z), F32),
            pltpu.VMEM((3, 1, share), F32),
            pltpu.SemaphoreType.DMA((block_x,)),
            pltpu.SemaphoreType.DMA,
        ],
        name="step_cells",
    )(*in_vmem(*kept, near_in, far_in, message_in, *hots))
    return (state, new_motion)


def solution(mesh):
    placed = (
        P("slab", "col", None),
        P(None, "slab", "col", None),
        P("slab", "col", None),
        P("slab", "col", None),
        P("slab", "col", None),
        P("slab", "col", None),
        P("slab", "col"),
        P(None, "slab", "col", None),
        P("slab", None),
        P("slab", None),
        P(None, "slab", None),
    )
    return jax.shard_map(
        local,
        mesh=mesh,
        in_specs=placed,
        out_specs=(P(None, "slab", "col", None), P(None, "slab", "col")),
        check_vma=False,
    )
```

time: 109 us -> 29.5 us (0.27)
  the two profiles are of different devices: /device:TPU:16 before, /device:TPU:2 now
where the time goes in v1:
time: 29.5 us; the launch traced here: 29.3 us
  starting transfers between devices  13.5 us (46%)
  blocking collectives  10.8 us (37%)
  Pallas kernels  3.7 us (13%)
  between operations  1.3 us (4%)
    ppermute x1, starting transfers between devices, local(): far_in = lax.ppermute(far, 'slab', outer)  11.6 us
    all_to_all x1, blocking collectives, local(): message_in = lax.all_to_all(message, 'col', 0, 0)  10.8 us
    pallas_call x1, Pallas kernels, local(): pl.pallas_call(step_kernel, out_shape=(jax.ShapeDtypeStruct((5, block_x,...  2.06 us
    ppermute x1, starting transfers between devices, local(): near_in = lax.ppermute(near, 'slab', inner)  1.92 us
    pallas_call x1, Pallas kernels, local(): pl.pallas_call(gather_kernel, out_shape=tuple((pltpu.VMEM(array.shape, ar...  1.64 us
  transfers between devices with their start and end apart: 2, of which 0 were waited for; matrix products, arithmetic and copies ran while one was open for 0% of the time, Pallas kernels for 0%

profile of v1, /device:TPU:2, one launch (start us, length us, event | category | flops | bytes accessed | tf_op | source)
XLA Modules:
  0.0 29.3 jit_solution(453517815510744041)
XLA Ops:
  1.3 1.6 %gather_rows.1 = (f32[2,32,256]{2,1,0:T(8,128)S(1)}, f32[3,2,32,256]{3,2,1,0:T(8,128)S(1)}, f32[2,32,256]{2,1,0:T(8,128)S(1)}, s32[2,32,256]{2,1,0:T(8,128)S(1)}...) custom-call(s32[1,1]{1,0:T(1,128)S(6)} %copy.13.count_in, ...), custom_call_target="tpu_custom_call" | custom-call | tf_op jit(solution)/shard_map/gather_rows/pallas_call | solution.py:309
  2.9 1.9 %collective-permute-start = (f32[6,32,256]{2,1,0:T(8,128)S(1)}, f32[6,32,256]{2,1,0:T(8,128)S(1)}, u32[]{:S(2)}, u32[]{:S(2)}) collective-permute-start(f32[6,32,256]{2,1,0:T(8,128)S(1)} %get-tuple-element.25), channel_id=1, source_target_pairs={{0,4},{4,0},{8,12},{12,8},{16,20},{20,16},{24,28},{28,24},{32,36},... | collective-permute-start | bytes 589832 | tf_op jit(solution)/shard_map/ppermute | solution.py:340
  4.9 11.6 %collective-permute-start.1 = (f32[6,32,256]{2,1,0:T(8,128)S(1)}, f32[6,32,256]{2,1,0:T(8,128)S(1)}, u32[]{:S(2)}, u32[]{:S(2)}) collective-permute-start(f32[6,32,256]{2,1,0:T(8,128)S(1)} %get-tuple-element.26), channel_id=1, source_target_pairs={{4,8},{8,4},{12,16},{16,12},{20,24},{24,20},{28,32},{32,28},{36,40... | collective-permute-start | bytes 589832 | tf_op jit(solution)/shard_map/ppermute | solution.py:341
  16.4 10.8 %all_to_all.5.message = f32[4,24,256]{2,1,0:T(8,128)S(1)} all-to-all(f32[4,24,256]{2,1,0:T(8,128)S(1)} %get-tuple-element.27), channel_id=1, replica_groups=mesh['slab'=192,'col'=4] {'col'}, dimensions={0} | all-to-all | bytes 196608 | tf_op jit(solution)/shard_map/all_to_all | solution.py:342
  27.3 0.0 collective-permute-done.near_ref
  27.3 0.0 collective-permute-done.1.far_ref
  27.3 2.1 %step_cells.1 = (f32[5,2,32,256]{3,2,1,0:T(8,128)}, f32[3,1,128]{2,1,0:T(1,128)}) custom-call(f32[2,32,256]{2,1,0:T(8,128)S(1)} %get-tuple-element.17.density, f32[3,2,32,256]{3,2,1,0:T(8,128)S(1)} %get-tuple-element.18.velocity, f32[2,32,256]{2,1,0:T(8,128)S(1)} %get-tuple-element.19.pressure, s32[2,32,256]{2,1,0:T(8,128)S(1)} %get-tuple-element.20.code, ...), custom_call_target="tpu_custom_call" | custom-call | tf_op jit(solution)/shard_map/step_cells/pallas_call | solution.py:344
Async XLA Ops:
  2.9 24.3 %collective-permute-start = (f32[6,32,256]{2,1,0:T(8,128)S(1)}, f32[6,32,256]{2,1,0:T(8,128)S(1)}, u32[]{:S(2)}, u32[]{:S(2)}) collective-permute-start(f32[6,32,256]{2,1,0:T(8,128)S(1)} %get-tuple-element.25), channel_id=1, source_target_pairs={{0,4},{4,0},{8,12},{12,8},{16,20},{20,16},{24,28},{28,24},{32,36},... | collective-permute-start | bytes 589832 | tf_op jit(solution)/shard_map/ppermute | solution.py:340
  4.9 22.4 %collective-permute-start.1 = (f32[6,32,256]{2,1,0:T(8,128)S(1)}, f32[6,32,256]{2,1,0:T(8,128)S(1)}, u32[]{:S(2)}, u32[]{:S(2)}) collective-permute-start(f32[6,32,256]{2,1,0:T(8,128)S(1)} %get-tuple-element.26), channel_id=1, source_target_pairs={{4,8},{8,4},{12,16},{16,12},{20,24},{24,20},{28,32},{32,28},{36,40... | collective-permute-start | bytes 589832 | tf_op jit(solution)/shard_map/ppermute | solution.py:341

commit v2 on v1

--- a/solution.py
+++ b/solution.py
@@ -31,7 +31,7 @@
 
 def gather_kernel(count_in, cell_in, element_in, *refs):
     given, kept = refs[:8], refs[8:16]
-    near_ref, far_ref, message, weight_ref, third_hot, plane_hot, element_hot = refs[16:23]
+    far_ref, near_ref, message, weight_ref, third_hot, plane_hot, element_hot = refs[16:23]
     count, cell, element, sems = refs[23:]
     density, velocity, pressure, code, normal = kept[:5]
     pairs = [(cell_in, cell), (element_in, element), (count_in, count)] + list(zip(given, kept))
@@ -46,7 +46,7 @@
     odd = lax.rem(lax.axis_index("slab"), 2)
     col = lax.axis_index("col")
 
-    for target, at in ((near_ref, 1 - odd), (far_ref, odd)):
+    for target, at in ((far_ref, odd), (near_ref, 1 - odd)):
         target[0] = density[at]
         for k in range(3):
             target[1 + k] = velocity[k, at]
@@ -137,8 +137,8 @@
     mass,
     removed,
     motion,
+    far_ref,
     near_ref,
-    far_ref,
     message,
     weight_ref,
     third_hot,
@@ -333,12 +333,12 @@
         interface_element,
         *given,
     )
-    kept, (near, far, message), hots = results[:8], results[8:11], results[11:]
+    kept, (far, near, message), hots = results[:8], results[8:11], results[11:]
 
     inner = [(i, i ^ 1) for i in range(slabs)]
     outer = [(i, i + 1 if i % 2 else i - 1) for i in range(1, slabs - 1)]
+    far_in = lax.ppermute(far, "slab", outer)
     near_in = lax.ppermute(near, "slab", inner)
-    far_in = lax.ppermute(far, "slab", outer)
     message_in = lax.all_to_all(message, "col", 0, 0)
 
     state, new_motion = pl.pallas_call(
@@ -358,7 +358,7 @@
             pltpu.SemaphoreType.DMA,
         ],
         name="step_cells",
-    )(*in_vmem(*kept, near_in, far_in, message_in, *hots))
+    )(*in_vmem(*kept, far_in, near_in, message_in, *hots))
     return (state, new_motion)
 
 

time: 29.5 us -> 28.2 us (0.956)
  the two profiles are of different devices: /device:TPU:2 before, /device:TPU:512 now
where the time goes in v2:
time: 28.2 us; the launch traced here: 28 us
  blocking collectives  14.7 us (52%)
  starting transfers between devices  8.24 us (29%)
  Pallas kernels  3.7 us (13%)
  between operations  1.3 us (5%)
    all_to_all x1, blocking collectives, local(): message_in = lax.all_to_all(message, 'col', 0, 0)  14.7 us
    ppermute x1, starting transfers between devices, local(): far_in = lax.ppermute(far, 'slab', outer)  6.32 us
    pallas_call x1, Pallas kernels, local(): pl.pallas_call(step_kernel, out_shape=(jax.ShapeDtypeStruct((5, block_x,...  2.06 us
    ppermute x1, starting transfers between devices, local(): near_in = lax.ppermute(near, 'slab', inner)  1.92 us
    pallas_call x1, Pallas kernels, local(): pl.pallas_call(gather_kernel, out_shape=tuple((pltpu.VMEM(array.shape, ar...  1.64 us
  transfers between devices with their start and end apart: 2, of which 0 were waited for; matrix products, arithmetic and copies ran while one was open for 0% of the time, Pallas kernels for 0%

profile of v2, /device:TPU:512, one launch (start us, length us, event | category | flops | bytes accessed | tf_op | source)
XLA Modules:
  0.0 28.0 jit_solution(15855600906445695557)
XLA Ops:
  1.3 1.6 %gather_rows.1 = (f32[2,32,256]{2,1,0:T(8,128)S(1)}, f32[3,2,32,256]{3,2,1,0:T(8,128)S(1)}, f32[2,32,256]{2,1,0:T(8,128)S(1)}, s32[2,32,256]{2,1,0:T(8,128)S(1)}...) custom-call(s32[1,1]{1,0:T(1,128)S(6)} %copy.13.count_in, ...), custom_call_target="tpu_custom_call" | custom-call | tf_op jit(solution)/shard_map/gather_rows/pallas_call | solution.py:309
  2.9 6.3 %collective-permute-start = (f32[6,32,256]{2,1,0:T(8,128)S(1)}, f32[6,32,256]{2,1,0:T(8,128)S(1)}, u32[]{:S(2)}, u32[]{:S(2)}) collective-permute-start(f32[6,32,256]{2,1,0:T(8,128)S(1)} %get-tuple-element.25), channel_id=1, source_target_pairs={{4,8},{8,4},{12,16},{16,12},{20,24},{24,20},{28,32},{32,28},{36,40... | collective-permute-start | bytes 589832 | tf_op jit(solution)/shard_map/ppermute | solution.py:340
  9.2 1.9 %collective-permute-start.1 = (f32[6,32,256]{2,1,0:T(8,128)S(1)}, f32[6,32,256]{2,1,0:T(8,128)S(1)}, u32[]{:S(2)}, u32[]{:S(2)}) collective-permute-start(f32[6,32,256]{2,1,0:T(8,128)S(1)} %get-tuple-element.26), channel_id=1, source_target_pairs={{0,4},{4,0},{8,12},{12,8},{16,20},{20,16},{24,28},{28,24},{32,36},... | collective-permute-start | bytes 589832 | tf_op jit(solution)/shard_map/ppermute | solution.py:341
  11.2 14.7 %all_to_all.5.message = f32[4,24,256]{2,1,0:T(8,128)S(1)} all-to-all(f32[4,24,256]{2,1,0:T(8,128)S(1)} %get-tuple-element.27), channel_id=1, replica_groups=mesh['slab'=192,'col'=4] {'col'}, dimensions={0} | all-to-all | bytes 196608 | tf_op jit(solution)/shard_map/all_to_all | solution.py:342
  25.9 0.0 collective-permute-done.far_ref
  25.9 0.0 collective-permute-done.1.near_ref
  25.9 2.1 %step_cells.1 = (f32[5,2,32,256]{3,2,1,0:T(8,128)}, f32[3,1,128]{2,1,0:T(1,128)}) custom-call(f32[2,32,256]{2,1,0:T(8,128)S(1)} %get-tuple-element.17.density, f32[3,2,32,256]{3,2,1,0:T(8,128)S(1)} %get-tuple-element.18.velocity, f32[2,32,256]{2,1,0:T(8,128)S(1)} %get-tuple-element.19.pressure, s32[2,32,256]{2,1,0:T(8,128)S(1)} %get-tuple-element.20.code, ...), custom_call_target="tpu_custom_call" | custom-call | tf_op jit(solution)/shard_map/step_cells/pallas_call | solution.py:344
Async XLA Ops:
  2.9 23.0 %collective-permute-start = (f32[6,32,256]{2,1,0:T(8,128)S(1)}, f32[6,32,256]{2,1,0:T(8,128)S(1)}, u32[]{:S(2)}, u32[]{:S(2)}) collective-permute-start(f32[6,32,256]{2,1,0:T(8,128)S(1)} %get-tuple-element.25), channel_id=1, source_target_pairs={{4,8},{8,4},{12,16},{16,12},{20,24},{24,20},{28,32},{32,28},{36,40... | collective-permute-start | bytes 589832 | tf_op jit(solution)/shard_map/ppermute | solution.py:340
  9.2 16.7 %collective-permute-start.1 = (f32[6,32,256]{2,1,0:T(8,128)S(1)}, f32[6,32,256]{2,1,0:T(8,128)S(1)}, u32[]{:S(2)}, u32[]{:S(2)}) collective-permute-start(f32[6,32,256]{2,1,0:T(8,128)S(1)} %get-tuple-element.26), channel_id=1, source_target_pairs={{0,4},{4,0},{8,12},{12,8},{16,20},{20,16},{24,28},{28,24},{32,36},... | collective-permute-start | bytes 589832 | tf_op jit(solution)/shard_map/ppermute | solution.py:341

commit v3 on v2

--- a/solution.py
+++ b/solution.py
@@ -31,8 +31,8 @@
 
 def gather_kernel(count_in, cell_in, element_in, *refs):
     given, kept = refs[:8], refs[8:16]
-    far_ref, near_ref, message, weight_ref, third_hot, plane_hot, element_hot = refs[16:23]
-    count, cell, element, sems = refs[23:]
+    message, weight_ref, third_hot, plane_hot, element_hot = refs[16:21]
+    count, cell, element, sems = refs[21:]
     density, velocity, pressure, code, normal = kept[:5]
     pairs = [(cell_in, cell), (element_in, element), (count_in, count)] + list(zip(given, kept))
     copies = [pltpu.make_async_copy(a, b, sems.at[i]) for i, (a, b) in enumerate(pairs)]
@@ -43,15 +43,7 @@
     block_x, block_y, block_z = density.shape
     rows = cell.shape[2]
     group = element_hot.shape[0]
-    odd = lax.rem(lax.axis_index("slab"), 2)
     col = lax.axis_index("col")
-
-    for target, at in ((far_ref, odd), (near_ref, 1 - odd)):
-        target[0] = density[at]
-        for k in range(3):
-            target[1 + k] = velocity[k, at]
-        target[4] = pressure[at]
-        target[5] = code[at].astype(F32) * (1.0 / 16.0)
 
     def edge(x, y):
         out = [density[x, y : y + 1]]
@@ -128,6 +120,78 @@
     return out
 
 
+def plane_kernel(density, velocity, pressure, code, far_ref, near_ref):
+    odd = lax.rem(lax.axis_index("slab"), 2)
+    for target, at in ((far_ref, odd), (near_ref, 1 - odd)):
+        target[0] = density[at]
+        for k in range(3):
+            target[1 + k] = velocity[k, at]
+        target[4] = pressure[at]
+        target[5] = code[at].astype(F32) * (1.0 / 16.0)
+
+
+def inner_kernel(density, velocity, pressure, code, total, terms):
+    block_x, block_y, block_z = density.shape
+    lane = lax.broadcasted_iota(I32, (TILE, block_z), 1)
+    row = lax.broadcasted_iota(I32, (TILE, block_z), 0)
+    tiles = block_y // TILE
+
+    def prims(x, t):
+        at = slice(t * TILE, (t + 1) * TILE)
+        out = [density[x, at]] + [velocity[k, x, at] for k in range(3)]
+        return out + [pressure[x, at], code[x, at].astype(F32) * (1.0 / 16.0)]
+
+    def shifted(value, after):
+        return jnp.where(row == TILE - 1, pltpu.roll(after, TILE - 1, 0), pltpu.roll(value, TILE - 1, 0))
+
+    def full(x, t):
+        own = prims(x, t)
+        return dict(enumerate(own + list(derive(*own[:5]))))
+
+    def keep(x, t, own):
+        at = slice(t * TILE, (t + 1) * TILE)
+        for i, name in enumerate((M0, M1, M2, ENE, SND)):
+            terms[i, x, at] = own[name]
+
+    for t in range(tiles):
+        low, high = full(0, t), full(1, t)
+        keep(0, t, low)
+        keep(1, t, high)
+        across = face(0, low, high)
+        at = slice(t * TILE, (t + 1) * TILE)
+        for x, own in ((0, low), (1, high)):
+            right = {name: pltpu.roll(value, block_z - 1, 1) for name, value in own.items()}
+            right[FRAC] = jnp.where(lane == block_z - 1, 0.0, right[FRAC])
+            upper = face(2, own, right)
+            for i in range(5):
+                value = upper[i] - pltpu.roll(upper[i], 1, 1)
+                total[i, x, at] = value + across[i] if x == 0 else value - across[i]
+    for x in range(block_x):
+        before = None
+        for t in range(tiles):
+            at = slice(t * TILE, (t + 1) * TILE)
+
+            def load(u):
+                at = slice(u * TILE, (u + 1) * TILE)
+                out = {RHO: density[x, at], V1: velocity[1, x, at], PRS: pressure[x, at]}
+                out[FRAC] = code[x, at].astype(F32) * (1.0 / 16.0)
+                for i, name in enumerate((M0, M1, M2, ENE, SND)):
+                    out[name] = terms[i, x, at]
+                return out
+
+            own = load(t)
+            after = load(min(t + 1, tiles - 1))
+            above = {name: shifted(own[name], after[name]) for name in own}
+            if t == tiles - 1:
+                above[FRAC] = jnp.where(row == TILE - 1, 0.0, above[FRAC])
+            upper = face(1, own, above)
+            turned = [pltpu.roll(value, 1, 0) for value in upper]
+            for i in range(5):
+                first = jnp.zeros_like(turned[i]) if before is None else before[i]
+                total[i, x, at] += upper[i] - jnp.where(row == 0, first, turned[i])
+            before = turned
+
+
 def step_kernel(
     density,
     velocity,
@@ -137,6 +201,8 @@
     mass,
     removed,
     motion,
+    total,
+    terms,
     far_ref,
     near_ref,
     message,
@@ -146,7 +212,6 @@
     element_hot,
     state_out,
     motion_out,
-    cells,
     source,
     state,
     own_motion,
@@ -159,8 +224,7 @@
     cols = message.shape[0]
     odd = lax.rem(lax.axis_index("slab"), 2)
     col = lax.axis_index("col")
-    half = group // 2
-    pad = TILE
+    tiles = block_y // TILE
 
     keep = 1.0 - removed[...].astype(F32)
     new = []
@@ -200,72 +264,52 @@
             block_x, block_y, block_z
         )
 
-    def store(plane, at, count, prims, fraction):
-        full = list(prims) + [fraction] + list(derive(*prims))
-        for name, value in enumerate(full):
-            cells[name, plane, at : at + count] = value
-
+    def other(prims, fraction):
+        live = fraction > 0.0
+        prims = [jnp.where(live, prims[0], 1.0)] + prims[1:4] + [jnp.where(live, prims[4], 1.0)]
+        return dict(enumerate(prims + [fraction] + list(derive(*prims))))
+
+    def edge(along_y):
+        out = {RHO: density[:, along_y], PRS: pressure[:, along_y]}
+        for k in range(3):
+            out[V0 + k] = velocity[k, :, along_y]
+            out[M0 + k] = terms[k, :, along_y]
+        out[FRAC] = code[:, along_y].astype(F32) * (1.0 / 16.0)
+        out[ENE], out[SND] = terms[3, :, along_y], terms[4, :, along_y]
+        return out
+
+    def arrived(j, inside):
+        rows = [message[j, f * block_x : (f + 1) * block_x] for f in range(6)]
+        return other(rows[:5], jnp.where(inside, rows[5], 0.0))
+
+    bottom = face(1, arrived(jnp.maximum(col - 1, 0), col > 0), edge(0))
+    top = face(1, edge(block_y - 1), arrived(jnp.minimum(col + 1, cols - 1), col < cols - 1))
+
+    row = lax.broadcasted_iota(I32, (TILE, block_z), 0)
     for x in range(block_x):
-        for t in range(block_y // TILE):
+        for t in range(tiles):
             at = slice(t * TILE, (t + 1) * TILE)
-            prims = [density[x, at]] + [velocity[k, x, at] for k in range(3)] + [pressure[x, at]]
-            store(1 + x, pad + t * TILE, TILE, prims, code[x, at].astype(F32) * (1.0 / 16.0))
-    for ref, plane in ((near_ref, 3 * (1 - odd)), (far_ref, 3 * odd)):
-        for t in range(block_y // TILE):
-            at = slice(t * TILE, (t + 1) * TILE)
-            fraction = ref[5, at]
-            live = fraction > 0.0
-            prims = [jnp.where(live, ref[0, at], 1.0)] + [ref[1 + k, at] for k in range(3)]
-            prims.append(jnp.where(live, ref[4, at], 1.0))
-            store(plane, pad + t * TILE, TILE, prims, fraction)
-    for other, inside, at in (
-        (jnp.maximum(col - 1, 0), col > 0, pad - 1),
-        (jnp.minimum(col + 1, cols - 1), col < cols - 1, pad + block_y),
-    ):
-        for x in range(block_x):
-            prims = [message[other, f * block_x + x][None] for f in range(5)]
-            fraction = message[other, 5 * block_x + x][None]
-            store(1 + x, at, 1, prims, jnp.where(inside, fraction, 0.0))
-
-    lane = lax.broadcasted_iota(I32, (TILE, block_z), 1)
-    row = lax.broadcasted_iota(I32, (TILE, block_z), 0)
-
-    def load(plane, at, along):
-        out = {}
-        for name in (RHO, V0 + along, PRS, FRAC, M0, M1, M2, ENE, SND):
-            out[name] = cells[name, plane, at : at + TILE]
-        return out
-
-    for x in range(block_x):
-        before = None
-        for t in range(-1, block_y // TILE):
-            at = pad + t * TILE
-            upper = face(1, load(1 + x, at, 1), load(1 + x, at + 1, 1))
-            turned = [pltpu.roll(value, 1, 0) for value in upper]
-            if t < 0:
-                before = turned
-                continue
-            total = [
-                value - jnp.where(row == 0, old, fresh)
-                for value, old, fresh in zip(upper, before, turned)
-            ]
-            before = turned
-            own = load(1 + x, at, 2)
-            right = {name: pltpu.roll(value, block_z - 1, 1) for name, value in own.items()}
-            right[FRAC] = jnp.where(lane == block_z - 1, 0.0, right[FRAC])
-            upper = face(2, own, right)
-            total = [
-                value + (flux - pltpu.roll(flux, 1, 1)) for value, flux in zip(total, upper)
-            ]
-            own = load(1 + x, at, 0)
-            upper = face(0, own, load(2 + x, at, 0))
-            lower = face(0, load(x, at, 0), own)
-            total = [value + (u - v) for value, u, v in zip(total, upper, lower)]
+            near = [near_ref[f, at] for f in range(6)]
+            far = [far_ref[f, at] for f in range(6)]
+            use_near = odd == (1 - x)
+            got = [jnp.where(use_near, a, b) for a, b in zip(near, far)]
+            beyond = other(got[:5], got[5])
+            own = {RHO: density[x, at], PRS: pressure[x, at], V0: velocity[0, x, at]}
+            for k in range(3):
+                own[M0 + k] = terms[k, x, at]
+            own[FRAC] = code[x, at].astype(F32) * (1.0 / 16.0)
+            own[ENE], own[SND] = terms[3, x, at], terms[4, x, at]
+            flux = face(0, beyond, own) if x == 0 else face(0, own, beyond)
             scale = step_ratio / own[FRAC]
-            rows = slice(t * TILE, (t + 1) * TILE)
             for i, name in enumerate((RHO, M0, M1, M2, ENE)):
-                change = total[i] - source[i - 1, x, rows] if i else total[i]
-                state[i, x, rows] = own[name] - scale * change
+                change = total[i, x, at] - flux[i] if x == 0 else total[i, x, at] + flux[i]
+                if t == 0:
+                    change = change - jnp.where(row == 0, bottom[i][x : x + 1], 0.0)
+                if t == tiles - 1:
+                    change = change + jnp.where(row == TILE - 1, top[i][x : x + 1], 0.0)
+                if i:
+                    change = change - source[i - 1, x, at]
+                state[i, x, at] = own[name] - scale * change
         pltpu.make_async_copy(state.at[:, x], state_out.at[:, x], state_sem.at[x]).start()
     for x in range(block_x):
         pltpu.make_async_copy(state.at[:, x], state_out.at[:, x], state_sem.at[x]).wait()
@@ -310,8 +354,6 @@
         gather_kernel,
         out_shape=tuple(pltpu.VMEM(array.shape, array.dtype) for array in given)
         + (
-            pltpu.VMEM((6, block_y, block_z), F32),
-            pltpu.VMEM((6, block_y, block_z), F32),
             pltpu.VMEM((cols, 24, block_z), F32),
             pltpu.VMEM((1, rows), F32),
             pltpu.VMEM((block_z, rows), BF16),
@@ -319,7 +361,7 @@
             pltpu.VMEM((group, rows), BF16),
         ),
         in_specs=[pl.BlockSpec(memory_space=pl.ANY)] + [hbm] * 10,
-        out_specs=[vmem] * 15,
+        out_specs=[vmem] * 13,
         scratch_shapes=[
             pltpu.VMEM(interface_count.shape, I32),
             pltpu.VMEM(interface_cell.shape, I32),
@@ -333,13 +375,33 @@
         interface_element,
         *given,
     )
-    kept, (far, near, message), hots = results[:8], results[8:11], results[11:]
-
+    kept, message, hots = results[:8], results[8], results[9:]
+
+    message_in = lax.all_to_all(message, "col", 0, 0)
+    planes = pltpu.VMEM((6, block_y, block_z), F32)
+    far, near = pl.pallas_call(
+        plane_kernel,
+        out_shape=(planes, planes),
+        in_specs=[vmem] * 4,
+        out_specs=[vmem] * 2,
+        cost_estimate=pl.CostEstimate(flops=100000, bytes_accessed=100000, transcendentals=0),
+        name="pack_planes",
+    )(*in_vmem(*kept[:4]))
+    total, terms = pl.pallas_call(
+        inner_kernel,
+        out_shape=(
+            pltpu.VMEM((5, block_x, block_y, block_z), F32),
+            pltpu.VMEM((5, block_x, block_y, block_z), F32),
+        ),
+        in_specs=[vmem] * 4,
+        out_specs=[vmem] * 2,
+        cost_estimate=pl.CostEstimate(flops=10000000000, bytes_accessed=100000000, transcendentals=0),
+        name="inner_faces",
+    )(*in_vmem(*kept[:4]))
     inner = [(i, i ^ 1) for i in range(slabs)]
     outer = [(i, i + 1 if i % 2 else i - 1) for i in range(1, slabs - 1)]
     far_in = lax.ppermute(far, "slab", outer)
     near_in = lax.ppermute(near, "slab", inner)
-    message_in = lax.all_to_all(message, "col", 0, 0)
 
     state, new_motion = pl.pallas_call(
         step_kernel,
@@ -347,10 +409,9 @@
             jax.ShapeDtypeStruct((5, block_x, block_y, block_z), F32),
             jax.ShapeDtypeStruct((3, 1, share), F32),
         ),
-        in_specs=[vmem] * 15,
+        in_specs=[vmem] * 17,
         out_specs=[hbm, hbm],
         scratch_shapes=[
-            pltpu.VMEM((11, block_x + 2, block_y + 2 * TILE, block_z), F32),
             pltpu.VMEM((4, block_x, block_y, block_z), F32),
             pltpu.VMEM((5, block_x, block_y, block_z), F32),
             pltpu.VMEM((3, 1, share), F32),
@@ -358,7 +419,7 @@
             pltpu.SemaphoreType.DMA,
         ],
         name="step_cells",
-    )(*in_vmem(*kept, far_in, near_in, message_in, *hots))
+    )(*in_vmem(*kept, total, terms, far_in, near_in, message_in, *hots))
     return (state, new_motion)
 
 

time: 28.2 us -> 25.1 us (0.89)
  the two profiles are of different devices: /device:TPU:512 before, /device:TPU:16 now
where the time goes in v3:
time: 25.1 us; the launch traced here: 24.8 us
  starting transfers between devices  15.2 us (61%)
  Pallas kernels  4.35 us (17%)
  waiting for transfers between devices  3.91 us (16%)
  between operations  1.31 us (5%)
    all_to_all x1, starting transfers between devices, local(): message_in = lax.all_to_all(message, 'col', 0, 0)  12.6 us
    all_to_all x1, waiting for transfers between devices, local(): message_in = lax.all_to_all(message, 'col', 0, 0)  3.9 us
    pallas_call x1, Pallas kernels, local(): pl.pallas_call(gather_kernel, out_shape=tuple((pltpu.VMEM(array.shape, ar...  2.28 us
    ppermute x1, starting transfers between devices, local(): near_in = lax.ppermute(near, 'slab', inner)  1.92 us
    pallas_call x1, Pallas kernels, local(): pl.pallas_call(step_kernel, out_shape=(jax.ShapeDtypeStruct((5, block_x,...  1.46 us
    ppermute x1, starting transfers between devices, local(): far_in = lax.ppermute(far, 'slab', outer)  0.67 us
    pallas_call x1, Pallas kernels, local(): pl.pallas_call(inner_kernel, out_shape=(pltpu.VMEM((5, block_x, block_y,...  0.58 us
  transfers between devices with their start and end apart: 3, of which 1 were waited for; matrix products, arithmetic and copies ran while one was open for 0% of the time, Pallas kernels for 2%

profile of v3, /device:TPU:16, one launch (start us, length us, event | category | flops | bytes accessed | tf_op | source)
XLA Modules:
  0.0 24.8 jit_solution(14281595478600126168)
XLA Ops:
  1.3 2.3 %gather_rows.1 = (f32[2,32,256]{2,1,0:T(8,128)S(1)}, f32[3,2,32,256]{3,2,1,0:T(8,128)S(1)}, f32[2,32,256]{2,1,0:T(8,128)S(1)}, s32[2,32,256]{2,1,0:T(8,128)S(1)}...) custom-call(s32[1,1]{1,0:T(1,128)S(6)} %copy.13.count_in, ...), custom_call_target="tpu_custom_call" | custom-call | tf_op jit(solution)/shard_map/gather_rows/pallas_call | solution.py:353
  3.6 12.6 %all-to-all-start = ((f32[4,24,256]{2,1,0:T(8,128)}), f32[4,24,256]{2,1,0:T(8,128)S(1)}, u32[]{:S(2)}, u32[]{:S(2)}) async-start(f32[4,24,256]{2,1,0:T(8,128)} %get-tuple-element.31), calls=%async_computation | async-start | bytes 196608 | tf_op jit(solution)/shard_map/all_to_all | solution.py:380
  16.2 0.7 %collective-permute-start = (f32[6,32,256]{2,1,0:T(8,128)S(1)}, f32[6,32,256]{2,1,0:T(8,128)S(1)}, u32[]{:S(2)}, u32[]{:S(2)}) collective-permute-start(f32[6,32,256]{2,1,0:T(8,128)S(1)} %get-tuple-element.29), channel_id=1, source_target_pairs={{4,8},{8,4},{12,16},{16,12},{20,24},{24,20},{28,32},{32,28},{36,40... | collective-permute-start | bytes 589832 | tf_op jit(solution)/shard_map/ppermute | solution.py:403
  16.9 1.9 %collective-permute-start.1 = (f32[6,32,256]{2,1,0:T(8,128)S(1)}, f32[6,32,256]{2,1,0:T(8,128)S(1)}, u32[]{:S(2)}, u32[]{:S(2)}) collective-permute-start(f32[6,32,256]{2,1,0:T(8,128)S(1)} %get-tuple-element.30), channel_id=1, source_target_pairs={{0,4},{4,0},{8,12},{12,8},{16,20},{20,16},{24,28},{28,24},{32,36},... | collective-permute-start | bytes 589832 | tf_op jit(solution)/shard_map/ppermute | solution.py:404
  18.8 0.6 %inner_faces.1 = (f32[5,2,32,256]{3,2,1,0:T(8,128)S(1)}, f32[5,2,32,256]{3,2,1,0:T(8,128)S(1)}) custom-call(f32[2,32,256]{2,1,0:T(8,128)S(1)} %get-tuple-element.19.density, f32[3,2,32,256]{3,2,1,0:T(8,128)S(1)} %get-tuple-element.20.velocity, f32[2,32,256]{2,1,0:T(8,128)S(1)} %get-tuple-element.21.pressure, s32[2,32,256]{2,1,0:T(8,128)S(1)} %get-tuple-element.22.code), custom_call_target="tpu_custom_call" | custom-call | flops 10000000000 | bytes 100000000 | tf_op jit(solution)/shard_map/inner_faces/pallas_call | solution.py:390
  19.4 3.9 %all-to-all-done.message = f32[4,24,256]{2,1,0:T(8,128)S(1)} async-done(((f32[4,24,256]{2,1,0:T(8,128)}), f32[4,24,256]{2,1,0:T(8,128)S(1)}, u32[]{:S(2)}, u32[]{:S(2)}) %all-to-all-start) | async-done | bytes 98336 | tf_op jit(solution)/shard_map/all_to_all | solution.py:380
  23.3 0.0 collective-permute-done.far_ref
  23.3 0.0 collective-permute-done.1.near_ref
  23.3 1.5 %step_cells.1 = (f32[5,2,32,256]{3,2,1,0:T(8,128)}, f32[3,1,128]{2,1,0:T(1,128)}) custom-call(f32[2,32,256]{2,1,0:T(8,128)S(1)} %get-tuple-element.19.density, f32[3,2,32,256]{3,2,1,0:T(8,128)S(1)} %get-tuple-element.20.velocity, f32[2,32,256]{2,1,0:T(8,128)S(1)} %get-tuple-element.21.pressure, s32[2,32,256]{2,1,0:T(8,128)S(1)} %get-tuple-element.22.code, ...), custom_call_target="tpu_custom_call" | custom-call | tf_op jit(solution)/shard_map/step_cells/pallas_call | solution.py:406
  (1 shorter events, 0.0 us)
Async XLA Ops:
  3.6 19.8 %all-to-all-start = ((f32[4,24,256]{2,1,0:T(8,128)}), f32[4,24,256]{2,1,0:T(8,128)S(1)}, u32[]{:S(2)}, u32[]{:S(2)}) async-start(f32[4,24,256]{2,1,0:T(8,128)} %get-tuple-element.31), calls=%async_computation | async-start | bytes 196608 | tf_op jit(solution)/shard_map/all_to_all | solution.py:380
  16.2 7.1 %collective-permute-start = (f32[6,32,256]{2,1,0:T(8,128)S(1)}, f32[6,32,256]{2,1,0:T(8,128)S(1)}, u32[]{:S(2)}, u32[]{:S(2)}) collective-permute-start(f32[6,32,256]{2,1,0:T(8,128)S(1)} %get-tuple-element.29), channel_id=1, source_target_pairs={{4,8},{8,4},{12,16},{16,12},{20,24},{24,20},{28,32},{32,28},{36,40... | collective-permute-start | bytes 589832 | tf_op jit(solution)/shard_map/ppermute | solution.py:403
  16.9 6.4 %collective-permute-start.1 = (f32[6,32,256]{2,1,0:T(8,128)S(1)}, f32[6,32,256]{2,1,0:T(8,128)S(1)}, u32[]{:S(2)}, u32[]{:S(2)}) collective-permute-start(f32[6,32,256]{2,1,0:T(8,128)S(1)} %get-tuple-element.30), channel_id=1, source_target_pairs={{0,4},{4,0},{8,12},{12,8},{16,20},{20,16},{24,28},{28,24},{32,36},... | collective-permute-start | bytes 589832 | tf_op jit(solution)/shard_map/ppermute | solution.py:404

commit v4 on v3

--- a/solution.py
+++ b/solution.py
@@ -34,32 +34,18 @@
     message, weight_ref, third_hot, plane_hot, element_hot = refs[16:21]
     count, cell, element, sems = refs[21:]
     density, velocity, pressure, code, normal = kept[:5]
-    pairs = [(cell_in, cell), (element_in, element), (count_in, count)] + list(zip(given, kept))
+    pairs = [(cell_in, cell), (element_in, element), (count_in, count)]
+    pairs += [(given[i], kept[i]) for i in (2, 3, 4, 0, 1, 5, 6, 7)]
     copies = [pltpu.make_async_copy(a, b, sems.at[i]) for i, (a, b) in enumerate(pairs)]
     for copy in copies:
         copy.start()
-    for copy in copies:
-        copy.wait()
     block_x, block_y, block_z = density.shape
     rows = cell.shape[2]
     group = element_hot.shape[0]
     col = lax.axis_index("col")
 
-    def edge(x, y):
-        out = [density[x, y : y + 1]]
-        out += [velocity[k, x, y : y + 1] for k in range(3)]
-        out += [pressure[x, y : y + 1], code[x, y : y + 1].astype(F32) * (1.0 / 16.0)]
-        return out
-
-    for x in range(block_x):
-        first, last = edge(x, 0), edge(x, block_y - 1)
-        for j in range(message.shape[0]):
-            for f in range(6):
-                at = f * block_x + x
-                message[j, at : at + 1] = jnp.where(col < j, last[f], first[f])
-
-    fraction = code[...].astype(F32) * (1.0 / 16.0)
-    table = (pressure[...] * (1.0 - fraction)).reshape(block_x * block_y, block_z)
+    copies[0].wait()
+    copies[1].wait()
     place = cell[0]
     third = jnp.bitwise_and(place, block_z - 1)
     plane = lax.shift_right_logical(place, block_z.bit_length() - 1)
@@ -69,6 +55,10 @@
     plane_hot[...] = jnp.where(plane_mask, 1.0, 0.0).astype(BF16)
     element_mask = lax.broadcasted_iota(I32, (group, rows), 0) == element[0]
     element_hot[...] = jnp.where(element_mask, 1.0, 0.0).astype(BF16)
+    for copy in copies[2:6]:
+        copy.wait()
+    fraction = code[...].astype(F32) * (1.0 / 16.0)
+    table = (pressure[...] * (1.0 - fraction)).reshape(block_x * block_y, block_z)
     parts = jnp.concatenate(split3(table), axis=0).astype(BF16)
     found = jnp.dot(parts, third_hot[...], preferred_element_type=F32)
     n = block_x * block_y
@@ -77,6 +67,21 @@
     live = lax.broadcasted_iota(I32, (1, rows), 1) < count[...]
     weight = jnp.where(live, found, 0.0)
     weight_ref[...] = weight
+
+    for copy in copies[6:]:
+        copy.wait()
+    def edge(x, y):
+        out = [density[x, y : y + 1]]
+        out += [velocity[k, x, y : y + 1] for k in range(3)]
+        out += [pressure[x, y : y + 1], code[x, y : y + 1].astype(F32) * (1.0 / 16.0)]
+        return out
+
+    for x in range(block_x):
+        first, last = edge(x, 0), edge(x, block_y - 1)
+        for j in range(message.shape[0]):
+            for f in range(6):
+                at = f * block_x + x
+                message[j, at : at + 1] = jnp.where(col < j, last[f], first[f])
 
     split = [split3(-weight * normal[k, 0]) for k in range(3)]
     force = stack_rows([split[k][i] for i in range(3) for k in range(3)], 16).astype(BF16)
@@ -130,7 +135,21 @@
         target[5] = code[at].astype(F32) * (1.0 / 16.0)
 
 
-def inner_kernel(density, velocity, pressure, code, total, terms):
+def scatter(hot, third_hot, row):
+    left = jnp.concatenate([hot * part.astype(BF16) for part in split3(row)], axis=0)
+    found = lax.dot_general(
+        left, third_hot[...], (((1,), (1,)), ((), ())), preferred_element_type=F32
+    )
+    n = hot.shape[0]
+    return found[:n] + found[n : 2 * n] + found[2 * n :]
+
+
+def inner_kernel(
+    density, velocity, pressure, code, normal, weight, third_hot, plane_hot, source, total, terms
+):
+    hot = plane_hot[...]
+    for k in range(3):
+        source[k] = scatter(hot, third_hot, weight[...] * normal[k, 0]).reshape(density.shape)
     block_x, block_y, block_z = density.shape
     lane = lax.broadcasted_iota(I32, (TILE, block_z), 1)
     row = lax.broadcasted_iota(I32, (TILE, block_z), 0)
@@ -201,6 +220,7 @@
     mass,
     removed,
     motion,
+    pushed,
     total,
     terms,
     far_ref,
@@ -246,23 +266,10 @@
     moved = jnp.dot(stacked, element_hot[...], preferred_element_type=F32)
     weight = weight_ref[...]
     work = jnp.zeros_like(weight)
-    values = []
     for k in range(3):
         row = moved[k : k + 1] + moved[3 + k : 4 + k] + moved[6 + k : 7 + k]
         work = work + normal[k, 0] * row
-        values.append(weight * normal[k, 0])
-    values.append(weight * work)
-    hot = plane_hot[...]
-    parts = [split3(value) for value in values]
-    for k in range(4):
-        left = jnp.concatenate([hot * parts[k][i].astype(BF16) for i in range(3)], axis=0)
-        found = lax.dot_general(
-            left, third_hot[...], (((1,), (1,)), ((), ())), preferred_element_type=F32
-        )
-        n = block_x * block_y
-        source[k] = (found[:n] + found[n : 2 * n] + found[2 * n :]).reshape(
-            block_x, block_y, block_z
-        )
+    source[...] = scatter(plane_hot[...], third_hot, weight * work).reshape(source.shape)
 
     def other(prims, fraction):
         live = fraction > 0.0
@@ -308,7 +315,7 @@
                 if t == tiles - 1:
                     change = change + jnp.where(row == TILE - 1, top[i][x : x + 1], 0.0)
                 if i:
-                    change = change - source[i - 1, x, at]
+                    change = change - (source[x, at] if i == 4 else pushed[i - 1, x, at])
                 state[i, x, at] = own[name] - scale * change
         pltpu.make_async_copy(state.at[:, x], state_out.at[:, x], state_sem.at[x]).start()
     for x in range(block_x):
@@ -387,17 +394,18 @@
         cost_estimate=pl.CostEstimate(flops=100000, bytes_accessed=100000, transcendentals=0),
         name="pack_planes",
     )(*in_vmem(*kept[:4]))
-    total, terms = pl.pallas_call(
+    pushed, total, terms = pl.pallas_call(
         inner_kernel,
         out_shape=(
+            pltpu.VMEM((3, block_x, block_y, block_z), F32),
             pltpu.VMEM((5, block_x, block_y, block_z), F32),
             pltpu.VMEM((5, block_x, block_y, block_z), F32),
         ),
-        in_specs=[vmem] * 4,
-        out_specs=[vmem] * 2,
+        in_specs=[vmem] * 8,
+        out_specs=[vmem] * 3,
         cost_estimate=pl.CostEstimate(flops=10000000000, bytes_accessed=100000000, transcendentals=0),
         name="inner_faces",
-    )(*in_vmem(*kept[:4]))
+    )(*in_vmem(*kept[:5], *hots[:3]))
     inner = [(i, i ^ 1) for i in range(slabs)]
     outer = [(i, i + 1 if i % 2 else i - 1) for i in range(1, slabs - 1)]
     far_in = lax.ppermute(far, "slab", outer)
@@ -409,17 +417,17 @@
             jax.ShapeDtypeStruct((5, block_x, block_y, block_z), F32),
             jax.ShapeDtypeStruct((3, 1, share), F32),
         ),
-        in_specs=[vmem] * 17,
+        in_specs=[vmem] * 18,
         out_specs=[hbm, hbm],
         scratch_shapes=[
-            pltpu.VMEM((4, block_x, block_y, block_z), F32),
+            pltpu.VMEM((block_x, block_y, block_z), F32),
             pltpu.VMEM((5, block_x, block_y, block_z), F32),
             pltpu.VMEM((3, 1, share), F32),
             pltpu.SemaphoreType.DMA((block_x,)),
             pltpu.SemaphoreType.DMA,
         ],
         name="step_cells",
-    )(*in_vmem(*kept, total, terms, far_in, near_in, message_in, *hots))
+    )(*in_vmem(*kept, pushed, total, terms, far_in, near_in, message_in, *hots))
     return (state, new_motion)
 
 

time: 25.1 us -> 24.8 us (0.988)
  transfers between devices with their start and end apart: 3 -> 3, of which waited for: 1 -> 1; matrix products, arithmetic and copies ran while one was open for 0% -> 0% of each run, Pallas kernels for 2% -> 3%
where the time goes in v4:
time: 24.8 us; the launch traced here: 24.5 us
  starting transfers between devices  15.2 us (61%)
  Pallas kernels  4.16 us (17%)
  waiting for transfers between devices  3.8 us (15%)
  between operations  1.31 us (5%)
    all_to_all x1, starting transfers between devices, local(): message_in = lax.all_to_all(message, 'col', 0, 0)  12.6 us
    all_to_all x1, waiting for transfers between devices, local(): message_in = lax.all_to_all(message, 'col', 0, 0)  3.8 us
    pallas_call x1, Pallas kernels, local(): pl.pallas_call(gather_kernel, out_shape=tuple((pltpu.VMEM(array.shape, ar...  2.15 us
    ppermute x1, starting transfers between devices, local(): near_in = lax.ppermute(near, 'slab', inner)  1.92 us
    pallas_call x1, Pallas kernels, local(): pl.pallas_call(step_kernel, out_shape=(jax.ShapeDtypeStruct((5, block_x,...  1.31 us
    pallas_call x1, Pallas kernels, local(): pl.pallas_call(inner_kernel, out_shape=(pltpu.VMEM((3, block_x, block_y,...  0.68 us
    ppermute x1, starting transfers between devices, local(): far_in = lax.ppermute(far, 'slab', outer)  0.67 us
  transfers between devices with their start and end apart: 3, of which 1 were waited for; matrix products, arithmetic and copies ran while one was open for 0% of the time, Pallas kernels for 3%

profile of v4, /device:TPU:16, one launch (start us, length us, event | category | flops | bytes accessed | tf_op | source)
XLA Modules:
  0.0 24.5 jit_solution(18073777217439492548)
XLA Ops:
  1.3 2.1 %gather_rows.1 = (f32[2,32,256]{2,1,0:T(8,128)S(1)}, f32[3,2,32,256]{3,2,1,0:T(8,128)S(1)}, f32[2,32,256]{2,1,0:T(8,128)S(1)}, s32[2,32,256]{2,1,0:T(8,128)S(1)}...) custom-call(s32[1,1]{1,0:T(1,128)S(6)} %copy.13.count_in, ...), custom_call_target="tpu_custom_call" | custom-call | tf_op jit(solution)/shard_map/gather_rows/pallas_call | solution.py:360
  3.4 12.6 %all-to-all-start = ((f32[4,24,256]{2,1,0:T(8,128)}), f32[4,24,256]{2,1,0:T(8,128)S(1)}, u32[]{:S(2)}, u32[]{:S(2)}) async-start(f32[4,24,256]{2,1,0:T(8,128)} %get-tuple-element.36), calls=%async_computation | async-start | bytes 196608 | tf_op jit(solution)/shard_map/all_to_all | solution.py:387
  16.1 0.7 %collective-permute-start = (f32[6,32,256]{2,1,0:T(8,128)S(1)}, f32[6,32,256]{2,1,0:T(8,128)S(1)}, u32[]{:S(2)}, u32[]{:S(2)}) collective-permute-start(f32[6,32,256]{2,1,0:T(8,128)S(1)} %get-tuple-element.34), channel_id=1, source_target_pairs={{4,8},{8,4},{12,16},{16,12},{20,24},{24,20},{28,32},{32,28},{36,40... | collective-permute-start | bytes 589832 | tf_op jit(solution)/shard_map/ppermute | solution.py:411
  16.8 1.9 %collective-permute-start.1 = (f32[6,32,256]{2,1,0:T(8,128)S(1)}, f32[6,32,256]{2,1,0:T(8,128)S(1)}, u32[]{:S(2)}, u32[]{:S(2)}) collective-permute-start(f32[6,32,256]{2,1,0:T(8,128)S(1)} %get-tuple-element.35), channel_id=1, source_target_pairs={{0,4},{4,0},{8,12},{12,8},{16,20},{20,16},{24,28},{28,24},{32,36},... | collective-permute-start | bytes 589832 | tf_op jit(solution)/shard_map/ppermute | solution.py:412
  18.7 0.7 %inner_faces.1 = (f32[3,2,32,256]{3,2,1,0:T(8,128)S(1)}, f32[5,2,32,256]{3,2,1,0:T(8,128)S(1)}, f32[5,2,32,256]{3,2,1,0:T(8,128)S(1)}) custom-call(f32[2,32,256]{2,1,0:T(8,128)S(1)} %get-tuple-element.20.density, f32[3,2,32,256]{3,2,1,0:T(8,128)S(1)} %get-tuple-element.21.velocity, f32[2,32,256]{2,1,0:T(8,128)S(1)} %get-tuple-element.22.pressure, ...), custom_call_target="tpu_custom_call" | custom-call | flops 10000000000 | bytes 100000000 | tf_op jit(solution)/shard_map/inner_faces/pallas_call | solution.py:397
  19.4 3.8 %all-to-all-done.message = f32[4,24,256]{2,1,0:T(8,128)S(1)} async-done(((f32[4,24,256]{2,1,0:T(8,128)}), f32[4,24,256]{2,1,0:T(8,128)S(1)}, u32[]{:S(2)}, u32[]{:S(2)}) %all-to-all-start) | async-done | bytes 98336 | tf_op jit(solution)/shard_map/all_to_all | solution.py:387
  23.2 0.0 collective-permute-done.far_ref
  23.2 0.0 collective-permute-done.1.near_ref
  23.2 1.3 %step_cells.1 = (f32[5,2,32,256]{3,2,1,0:T(8,128)}, f32[3,1,128]{2,1,0:T(1,128)}) custom-call(f32[2,32,256]{2,1,0:T(8,128)S(1)} %get-tuple-element.20.density, f32[3,2,32,256]{3,2,1,0:T(8,128)S(1)} %get-tuple-element.21.velocity, f32[2,32,256]{2,1,0:T(8,128)S(1)} %get-tuple-element.22.pressure, s32[2,32,256]{2,1,0:T(8,128)S(1)} %get-tuple-element.23.code, ...), custom_call_target="tpu_custom_call" | custom-call | tf_op jit(solution)/shard_map/step_cells/pallas_call | solution.py:414
  (1 shorter events, 0.0 us)
Async XLA Ops:
  3.4 19.8 %all-to-all-start = ((f32[4,24,256]{2,1,0:T(8,128)}), f32[4,24,256]{2,1,0:T(8,128)S(1)}, u32[]{:S(2)}, u32[]{:S(2)}) async-start(f32[4,24,256]{2,1,0:T(8,128)} %get-tuple-element.36), calls=%async_computation | async-start | bytes 196608 | tf_op jit(solution)/shard_map/all_to_all | solution.py:387
  16.1 7.1 %collective-permute-start = (f32[6,32,256]{2,1,0:T(8,128)S(1)}, f32[6,32,256]{2,1,0:T(8,128)S(1)}, u32[]{:S(2)}, u32[]{:S(2)}) collective-permute-start(f32[6,32,256]{2,1,0:T(8,128)S(1)} %get-tuple-element.34), channel_id=1, source_target_pairs={{4,8},{8,4},{12,16},{16,12},{20,24},{24,20},{28,32},{32,28},{36,40... | collective-permute-start | bytes 589832 | tf_op jit(solution)/shard_map/ppermute | solution.py:411
  16.8 6.4 %collective-permute-start.1 = (f32[6,32,256]{2,1,0:T(8,128)S(1)}, f32[6,32,256]{2,1,0:T(8,128)S(1)}, u32[]{:S(2)}, u32[]{:S(2)}) collective-permute-start(f32[6,32,256]{2,1,0:T(8,128)S(1)} %get-tuple-element.35), channel_id=1, source_target_pairs={{0,4},{4,0},{8,12},{12,8},{16,20},{20,16},{24,28},{28,24},{32,36},... | collective-permute-start | bytes 589832 | tf_op jit(solution)/shard_map/ppermute | solution.py:412

commit v5 on v4

--- a/solution.py
+++ b/solution.py
@@ -10,8 +10,11 @@
 struct_step = 1.0
 
 F32, BF16, I32 = jnp.float32, jnp.bfloat16, jnp.int32
+VMEM_BYTES = 8 * 2**20
 TILE = 8
-LOADS_AT = 16
+LANES = 128
+LOADS_AT = 24
+MESSAGE_ROWS = 40
 
 
 def split3(value):
@@ -31,8 +34,8 @@
 
 def gather_kernel(count_in, cell_in, element_in, *refs):
     given, kept = refs[:8], refs[8:16]
-    message, weight_ref, third_hot, plane_hot, element_hot = refs[16:21]
-    count, cell, element, sems = refs[21:]
+    message_out, weight_ref, third_hot, plane_hot, element_hot = refs[16:21]
+    count, cell, element, message, sems, sent = refs[21:]
     density, velocity, pressure, code, normal = kept[:5]
     pairs = [(cell_in, cell), (element_in, element), (count_in, count)]
     pairs += [(given[i], kept[i]) for i in (2, 3, 4, 0, 1, 5, 6, 7)]
@@ -80,21 +83,33 @@
         first, last = edge(x, 0), edge(x, block_y - 1)
         for j in range(message.shape[0]):
             for f in range(6):
-                at = f * block_x + x
-                message[j, at : at + 1] = jnp.where(col < j, last[f], first[f])
+                row = jnp.where(col < j, last[f], first[f])
+                for h in range(2):
+                    at = (2 * f + h) * block_x + x
+                    message[j, at : at + 1] = row[:, h * LANES : (h + 1) * LANES]
+    for j in range(message.shape[0]):
+        message[j, LOADS_AT + 12 :] = jnp.zeros((4, LANES), F32)
+    edges = slice(0, LOADS_AT)
+    edge_copy = pltpu.make_async_copy(message.at[:, edges], message_out.at[:, edges], sent.at[0])
+    edge_copy.start()
 
     split = [split3(-weight * normal[k, 0]) for k in range(3)]
     force = stack_rows([split[k][i] for i in range(3) for k in range(3)], 16).astype(BF16)
     partial = lax.dot_general(
         force, element_hot[...], (((1,), (1,)), ((), ())), preferred_element_type=F32
     )
-    half = group // 2
+    quarters = group // LANES
     for k in range(3):
         total = partial[k : k + 1] + partial[3 + k : 4 + k] + partial[6 + k : 7 + k]
-        for h in range(2):
-            at = LOADS_AT + 2 * k + h
+        for q in range(quarters):
+            at = LOADS_AT + quarters * k + q
             for j in range(message.shape[0]):
-                message[j, at : at + 1] = total[:, h * half : (h + 1) * half]
+                message[j, at : at + 1] = total[:, q * LANES : (q + 1) * LANES]
+    loads = slice(LOADS_AT, MESSAGE_ROWS)
+    load_copy = pltpu.make_async_copy(message.at[:, loads], message_out.at[:, loads], sent.at[1])
+    load_copy.start()
+    edge_copy.wait()
+    load_copy.wait()
 
 
 def derive(density, v0, v1, v2, pressure):
@@ -211,6 +226,38 @@
             before = turned
 
 
+def other(prims, fraction):
+    live = fraction > 0.0
+    prims = [jnp.where(live, prims[0], 1.0)] + prims[1:4] + [jnp.where(live, prims[4], 1.0)]
+    return dict(enumerate(prims + [fraction] + list(derive(*prims))))
+
+
+def outer_kernel(
+    density, velocity, pressure, code, pushed, total, terms, far_ref, near_ref, most, scale_ref
+):
+    block_x, block_y, block_z = density.shape
+    odd = lax.rem(lax.axis_index("slab"), 2)
+    for x in range(block_x):
+        use_near = odd == (1 - x)
+        for t in range(block_y // TILE):
+            at = slice(t * TILE, (t + 1) * TILE)
+            got = [jnp.where(use_near, near_ref[f, at], far_ref[f, at]) for f in range(6)]
+            beyond = other(got[:5], got[5])
+            own = {RHO: density[x, at], PRS: pressure[x, at], V0: velocity[0, x, at]}
+            for k in range(3):
+                own[M0 + k] = terms[k, x, at]
+            own[FRAC] = code[x, at].astype(F32) * (1.0 / 16.0)
+            own[ENE], own[SND] = terms[3, x, at], terms[4, x, at]
+            flux = face(0, beyond, own) if x == 0 else face(0, own, beyond)
+            scale = step_ratio / own[FRAC]
+            scale_ref[x, at] = scale
+            for i, name in enumerate((RHO, M0, M1, M2, ENE)):
+                change = total[i, x, at] - flux[i] if x == 0 else total[i, x, at] + flux[i]
+                if 0 < i < 4:
+                    change = change - pushed[i - 1, x, at]
+                most[i, x, at] = own[name] - scale * change
+
+
 def step_kernel(
     density,
     velocity,
@@ -220,11 +267,9 @@
     mass,
     removed,
     motion,
-    pushed,
-    total,
     terms,
-    far_ref,
-    near_ref,
+    most,
+    scale_ref,
     message,
     weight_ref,
     third_hot,
@@ -232,49 +277,45 @@
     element_hot,
     state_out,
     motion_out,
-    source,
     state,
     own_motion,
-    state_sem,
-    motion_sem,
+    sems,
 ):
     block_x, block_y, block_z = density.shape
     group = mass.shape[1]
     share = motion_out.shape[2]
     cols = message.shape[0]
-    odd = lax.rem(lax.axis_index("slab"), 2)
     col = lax.axis_index("col")
     tiles = block_y // TILE
+    copies = []
+
+    def send(source, target):
+        copies.append(pltpu.make_async_copy(source, target, sems.at[len(copies)]))
+        copies[-1].start()
+
+    for x in range(block_x):
+        at = slice(TILE, block_y - TILE)
+        send(most.at[0:4, x, at], state_out.at[0:4, x, at])
 
     keep = 1.0 - removed[...].astype(F32)
+    quarters = group // LANES
+    rows = slice(LOADS_AT, MESSAGE_ROWS)
+    loads = message[0, rows]
+    for j in range(1, cols):
+        loads = loads + message[j, rows]
     new = []
     for k in range(3):
-        at = LOADS_AT + 2 * k
-        load = message[0, at : at + 2]
-        for j in range(1, cols):
-            load = load + message[j, at : at + 2]
-        load = jnp.concatenate([load[0:1], load[1:2]], axis=1)
+        at = quarters * k
+        load = jnp.concatenate([loads[at + q : at + q + 1] for q in range(quarters)], axis=1)
         new.append((motion[k] + struct_step * load / mass[...]) * keep)
-        own = new[k][:, 0:share]
-        for j in range(1, cols):
-            own = jnp.where(col == j, new[k][:, j * share : (j + 1) * share], own)
-        own_motion[k] = own
-    motion_copy = pltpu.make_async_copy(own_motion, motion_out, motion_sem)
-    motion_copy.start()
     split = [split3(value) for value in new]
     stacked = stack_rows([split[k][i] for i in range(3) for k in range(3)], 16).astype(BF16)
     moved = jnp.dot(stacked, element_hot[...], preferred_element_type=F32)
-    weight = weight_ref[...]
-    work = jnp.zeros_like(weight)
+    work = jnp.zeros_like(weight_ref[...])
     for k in range(3):
         row = moved[k : k + 1] + moved[3 + k : 4 + k] + moved[6 + k : 7 + k]
         work = work + normal[k, 0] * row
-    source[...] = scatter(plane_hot[...], third_hot, weight * work).reshape(source.shape)
-
-    def other(prims, fraction):
-        live = fraction > 0.0
-        prims = [jnp.where(live, prims[0], 1.0)] + prims[1:4] + [jnp.where(live, prims[4], 1.0)]
-        return dict(enumerate(prims + [fraction] + list(derive(*prims))))
+    found = scatter(plane_hot[...], third_hot, weight_ref[...] * work)
 
     def edge(along_y):
         out = {RHO: density[:, along_y], PRS: pressure[:, along_y]}
@@ -286,45 +327,54 @@
         return out
 
     def arrived(j, inside):
-        rows = [message[j, f * block_x : (f + 1) * block_x] for f in range(6)]
-        return other(rows[:5], jnp.where(inside, rows[5], 0.0))
+        got = []
+        for f in range(6):
+            at = 2 * f * block_x
+            low, high = message[j, at : at + block_x], message[j, at + block_x : at + 2 * block_x]
+            got.append(jnp.concatenate([low, high], axis=1))
+        return other(got[:5], jnp.where(inside, got[5], 0.0))
 
     bottom = face(1, arrived(jnp.maximum(col - 1, 0), col > 0), edge(0))
     top = face(1, edge(block_y - 1), arrived(jnp.minimum(col + 1, cols - 1), col < cols - 1))
-
     row = lax.broadcasted_iota(I32, (TILE, block_z), 0)
+
+    def corrected(i, x, t):
+        at = slice(t * TILE, (t + 1) * TILE)
+        value = most[i, x, at]
+        if t == 0:
+            value = value + jnp.where(row == 0, scale_ref[x, at] * bottom[i][x : x + 1], 0.0)
+        if t == tiles - 1:
+            value = value - jnp.where(row == TILE - 1, scale_ref[x, at] * top[i][x : x + 1], 0.0)
+        return value
+
+    for x in range(block_x):
+        for t in (0, tiles - 1):
+            at = slice(t * TILE, (t + 1) * TILE)
+            for i in range(4):
+                state[i, x, at] = corrected(i, x, t)
+            send(state.at[0:4, x, at], state_out.at[0:4, x, at])
+    for k in range(3):
+        own = new[k][:, 0:share]
+        for j in range(1, cols):
+            own = jnp.where(col == j, new[k][:, j * share : (j + 1) * share], own)
+        own_motion[k] = own
+    send(own_motion, motion_out)
     for x in range(block_x):
         for t in range(tiles):
             at = slice(t * TILE, (t + 1) * TILE)
-            near = [near_ref[f, at] for f in range(6)]
-            far = [far_ref[f, at] for f in range(6)]
-            use_near = odd == (1 - x)
-            got = [jnp.where(use_near, a, b) for a, b in zip(near, far)]
-            beyond = other(got[:5], got[5])
-            own = {RHO: density[x, at], PRS: pressure[x, at], V0: velocity[0, x, at]}
-            for k in range(3):
-                own[M0 + k] = terms[k, x, at]
-            own[FRAC] = code[x, at].astype(F32) * (1.0 / 16.0)
-            own[ENE], own[SND] = terms[3, x, at], terms[4, x, at]
-            flux = face(0, beyond, own) if x == 0 else face(0, own, beyond)
-            scale = step_ratio / own[FRAC]
-            for i, name in enumerate((RHO, M0, M1, M2, ENE)):
-                change = total[i, x, at] - flux[i] if x == 0 else total[i, x, at] + flux[i]
-                if t == 0:
-                    change = change - jnp.where(row == 0, bottom[i][x : x + 1], 0.0)
-                if t == tiles - 1:
-                    change = change + jnp.where(row == TILE - 1, top[i][x : x + 1], 0.0)
-                if i:
-                    change = change - (source[x, at] if i == 4 else pushed[i - 1, x, at])
-                state[i, x, at] = own[name] - scale * change
-        pltpu.make_async_copy(state.at[:, x], state_out.at[:, x], state_sem.at[x]).start()
-    for x in range(block_x):
-        pltpu.make_async_copy(state.at[:, x], state_out.at[:, x], state_sem.at[x]).wait()
-    motion_copy.wait()
+            first = x * block_y + t * TILE
+            state[4, x, at] = corrected(4, x, t) + scale_ref[x, at] * found[first : first + TILE]
+    send(state.at[4], state_out.at[4])
+    for copy in copies:
+        copy.wait()
 
 
 def in_vmem(*arrays):
     return [pltpu.with_memory_space_constraint(array, pltpu.VMEM) for array in arrays]
+
+
+def in_hbm(*arrays):
+    return [pltpu.with_memory_space_constraint(array, pltpu.HBM) for array in arrays]
 
 
 def local(
@@ -361,26 +411,27 @@
         gather_kernel,
         out_shape=tuple(pltpu.VMEM(array.shape, array.dtype) for array in given)
         + (
-            pltpu.VMEM((cols, 24, block_z), F32),
+            jax.ShapeDtypeStruct((cols, MESSAGE_ROWS, LANES), F32),
             pltpu.VMEM((1, rows), F32),
             pltpu.VMEM((block_z, rows), BF16),
             pltpu.VMEM((block_x * block_y, rows), BF16),
             pltpu.VMEM((group, rows), BF16),
         ),
         in_specs=[pl.BlockSpec(memory_space=pl.ANY)] + [hbm] * 10,
-        out_specs=[vmem] * 13,
+        out_specs=[vmem] * 8 + [hbm] + [vmem] * 4,
         scratch_shapes=[
             pltpu.VMEM(interface_count.shape, I32),
             pltpu.VMEM(interface_cell.shape, I32),
             pltpu.VMEM(interface_element.shape, I32),
+            pltpu.VMEM((cols, MESSAGE_ROWS, LANES), F32),
             pltpu.SemaphoreType.DMA((11,)),
+            pltpu.SemaphoreType.DMA((2,)),
         ],
+        compiler_params=pltpu.CompilerParams(vmem_limit_bytes=VMEM_BYTES),
         name="gather_rows",
     )(
         interface_count,
-        interface_cell,
-        interface_element,
-        *given,
+        *in_hbm(interface_cell, interface_element, *given),
     )
     kept, message, hots = results[:8], results[8], results[9:]
 
@@ -392,6 +443,7 @@
         in_specs=[vmem] * 4,
         out_specs=[vmem] * 2,
         cost_estimate=pl.CostEstimate(flops=100000, bytes_accessed=100000, transcendentals=0),
+        compiler_params=pltpu.CompilerParams(vmem_limit_bytes=VMEM_BYTES),
         name="pack_planes",
     )(*in_vmem(*kept[:4]))
     pushed, total, terms = pl.pallas_call(
@@ -404,6 +456,7 @@
         in_specs=[vmem] * 8,
         out_specs=[vmem] * 3,
         cost_estimate=pl.CostEstimate(flops=10000000000, bytes_accessed=100000000, transcendentals=0),
+        compiler_params=pltpu.CompilerParams(vmem_limit_bytes=VMEM_BYTES),
         name="inner_faces",
     )(*in_vmem(*kept[:5], *hots[:3]))
     inner = [(i, i ^ 1) for i in range(slabs)]
@@ -411,23 +464,37 @@
     far_in = lax.ppermute(far, "slab", outer)
     near_in = lax.ppermute(near, "slab", inner)
 
+    cells = in_vmem(*kept[:4])
+    most, scale = pl.pallas_call(
+        outer_kernel,
+        out_shape=(
+            pltpu.VMEM((5, block_x, block_y, block_z), F32),
+            pltpu.VMEM((block_x, block_y, block_z), F32),
+        ),
+        in_specs=[vmem] * 9,
+        out_specs=[vmem] * 2,
+        cost_estimate=pl.CostEstimate(
+            flops=100 * density.size, bytes_accessed=64 * density.size, transcendentals=0
+        ),
+        compiler_params=pltpu.CompilerParams(vmem_limit_bytes=VMEM_BYTES),
+        name="outer_faces",
+    )(*cells, *in_vmem(pushed, total, terms, far_in, near_in))
     state, new_motion = pl.pallas_call(
         step_kernel,
         out_shape=(
             jax.ShapeDtypeStruct((5, block_x, block_y, block_z), F32),
             jax.ShapeDtypeStruct((3, 1, share), F32),
         ),
-        in_specs=[vmem] * 18,
+        in_specs=[vmem] * 16,
         out_specs=[hbm, hbm],
         scratch_shapes=[
-            pltpu.VMEM((block_x, block_y, block_z), F32),
             pltpu.VMEM((5, block_x, block_y, block_z), F32),
             pltpu.VMEM((3, 1, share), F32),
-            pltpu.SemaphoreType.DMA((block_x,)),
-            pltpu.SemaphoreType.DMA,
+            pltpu.SemaphoreType.DMA((3 * block_x + 2,)),
         ],
+        compiler_params=pltpu.CompilerParams(vmem_limit_bytes=VMEM_BYTES),
         name="step_cells",
-    )(*in_vmem(*kept, pushed, total, terms, far_in, near_in, message_in, *hots))
+    )(*in_vmem(*kept, terms, most, scale, message_in, *hots))
     return (state, new_motion)
 
 

time: 24.8 us -> 24.5 us (0.988)
  waiting for transfers between devices: 3.8 us -> 3.48 us
    all_to_all x1, waiting for transfers between devices: 3.8 us -> 2.75 us  [local(): message_in = lax.all_to_all(message, 'col', 0, 0)]
    ppermute x1, waiting for transfers between devices: 0.01 us -> 0.73 us  [local(): near_in = lax.ppermute(near, 'slab', inner)]
    pallas_call x0 -> x1, Pallas kernels: none -> 0.25 us  [local(): pl.pallas_call(outer_kernel, out_shape=(pltpu.VMEM((5, block_x, block_y,...]
  transfers between devices with their start and end apart: 3 -> 3, of which waited for: 1 -> 2; matrix products, arithmetic and copies ran while one was open for 0% -> 0% of each run, Pallas kernels for 3% -> 4%
where the time goes in v5:
time: 24.5 us; the launch traced here: 24.2 us
  starting transfers between devices  15.2 us (62%)
  Pallas kernels  4.18 us (17%)
  waiting for transfers between devices  3.48 us (14%)
  between operations  1.33 us (5%)
    all_to_all x1, starting transfers between devices, local(): message_in = lax.all_to_all(message, 'col', 0, 0)  12.6 us
    all_to_all x1, waiting for transfers between devices, local(): message_in = lax.all_to_all(message, 'col', 0, 0)  2.75 us
    pallas_call x1, Pallas kernels, local(): pl.pallas_call(gather_kernel, out_shape=tuple((pltpu.VMEM(array.shape, ar...  2.14 us
    ppermute x1, starting transfers between devices, local(): near_in = lax.ppermute(near, 'slab', inner)  1.92 us
    pallas_call x1, Pallas kernels, local(): pl.pallas_call(step_kernel, out_shape=(jax.ShapeDtypeStruct((5, block_x,...  1.11 us
    ppermute x1, waiting for transfers between devices, local(): near_in = lax.ppermute(near, 'slab', inner)  0.73 us
    ppermute x1, starting transfers between devices, local(): far_in = lax.ppermute(far, 'slab', outer)  0.67 us
    pallas_call x1, Pallas kernels, local(): pl.pallas_call(inner_kernel, out_shape=(pltpu.VMEM((3, block_x, block_y,...  0.66 us
  transfers between devices with their start and end apart: 3, of which 2 were waited for; matrix products, arithmetic and copies ran while one was open for 0% of the time, Pallas kernels for 4%

profile of v5, /device:TPU:16, one launch (start us, length us, event | category | flops | bytes accessed | tf_op | source)
XLA Modules:
  0.0 24.2 jit_solution(6666576992485579537)
XLA Ops:
  1.3 2.1 %gather_rows.1 = (f32[2,32,256]{2,1,0:T(8,128)S(1)}, f32[3,2,32,256]{3,2,1,0:T(8,128)S(1)}, f32[2,32,256]{2,1,0:T(8,128)S(1)}, s32[2,32,256]{2,1,0:T(8,128)S(1)}...) custom-call(s32[1,1]{1,0:T(1,128)S(6)} %copy.13.count_in, ...), custom_call_target="tpu_custom_call" | custom-call | tf_op jit(solution)/shard_map/gather_rows/pallas_call | solution.py:410
  3.4 12.6 %all-to-all-start = ((f32[4,40,128]{2,1,0:T(8,128)}), f32[4,40,128]{2,1,0:T(8,128)S(1)}, u32[]{:S(2)}, u32[]{:S(2)}) async-start(f32[4,40,128]{2,1,0:T(8,128)} %get-tuple-element.40), calls=%async_computation | async-start | bytes 163840 | tf_op jit(solution)/shard_map/all_to_all | solution.py:438
  16.1 0.7 %collective-permute-start = (f32[6,32,256]{2,1,0:T(8,128)S(1)}, f32[6,32,256]{2,1,0:T(8,128)S(1)}, u32[]{:S(2)}, u32[]{:S(2)}) collective-permute-start(f32[6,32,256]{2,1,0:T(8,128)S(1)} %get-tuple-element.36), channel_id=1, source_target_pairs={{4,8},{8,4},{12,16},{16,12},{20,24},{24,20},{28,32},{32,28},{36,40... | collective-permute-start | bytes 589832 | tf_op jit(solution)/shard_map/ppermute | solution.py:464
  16.8 1.9 %collective-permute-start.1 = (f32[6,32,256]{2,1,0:T(8,128)S(1)}, f32[6,32,256]{2,1,0:T(8,128)S(1)}, u32[]{:S(2)}, u32[]{:S(2)}) collective-permute-start(f32[6,32,256]{2,1,0:T(8,128)S(1)} %get-tuple-element.37), channel_id=1, source_target_pairs={{0,4},{4,0},{8,12},{12,8},{16,20},{20,16},{24,28},{28,24},{32,36},... | collective-permute-start | bytes 589832 | tf_op jit(solution)/shard_map/ppermute | solution.py:465
  18.7 0.7 %inner_faces.1 = (f32[3,2,32,256]{3,2,1,0:T(8,128)S(1)}, f32[5,2,32,256]{3,2,1,0:T(8,128)S(1)}, f32[5,2,32,256]{3,2,1,0:T(8,128)S(1)}) custom-call(f32[2,32,256]{2,1,0:T(8,128)S(1)} %get-tuple-element.22.density, f32[3,2,32,256]{3,2,1,0:T(8,128)S(1)} %get-tuple-element.23.velocity, f32[2,32,256]{2,1,0:T(8,128)S(1)} %get-tuple-element.24.pressure, ...), custom_call_target="tpu_custom_call" | custom-call | flops 10000000000 | bytes 100000000 | tf_op jit(solution)/shard_map/inner_faces/pallas_call | solution.py:449
  19.4 0.0 collective-permute-done.far_ref
  19.4 0.7 %collective-permute-done.1.near_ref = f32[6,32,256]{2,1,0:T(8,128)S(1)} collective-permute-done((f32[6,32,256]{2,1,0:T(8,128)S(1)}, f32[6,32,256]{2,1,0:T(8,128)S(1)}, u32[]{:S(2)}, u32[]{:S(2)}) %collective-permute-start.1) | collective-permute-done | bytes 196640 | tf_op jit(solution)/shard_map/ppermute | solution.py:465
  20.1 0.2 %outer_faces.1 = (f32[5,2,32,256]{3,2,1,0:T(8,128)S(1)}, f32[2,32,256]{2,1,0:T(8,128)S(1)}) custom-call(f32[2,32,256]{2,1,0:T(8,128)S(1)} %get-tuple-element.22.density, f32[3,2,32,256]{3,2,1,0:T(8,128)S(1)} %get-tuple-element.23.velocity, f32[2,32,256]{2,1,0:T(8,128)S(1)} %get-tuple-element.24.pressure, s32[2,32,256]{2,1,0:T(8,128)S(1)} %get-tuple-element.25.code, ...), custom_call_target="tpu_custom_call" | custom-call | flops 1638400 | bytes 1048576 | tf_op jit(solution)/shard_map/outer_faces/pallas_call | solution.py:468
  20.3 2.7 %all-to-all-done.message = f32[4,40,128]{2,1,0:T(8,128)S(1)} async-done(((f32[4,40,128]{2,1,0:T(8,128)}), f32[4,40,128]{2,1,0:T(8,128)S(1)}, u32[]{:S(2)}, u32[]{:S(2)}) %all-to-all-start) | async-done | bytes 81952 | tf_op jit(solution)/shard_map/all_to_all | solution.py:438
  23.1 1.1 %step_cells.1 = (f32[5,2,32,256]{3,2,1,0:T(8,128)}, f32[3,1,128]{2,1,0:T(1,128)}) custom-call(f32[2,32,256]{2,1,0:T(8,128)S(1)} %get-tuple-element.22.density, f32[3,2,32,256]{3,2,1,0:T(8,128)S(1)} %get-tuple-element.23.velocity, f32[2,32,256]{2,1,0:T(8,128)S(1)} %get-tuple-element.24.pressure, s32[2,32,256]{2,1,0:T(8,128)S(1)} %get-tuple-element.25.code, ...), custom_call_target="tpu_custom_call" | custom-call | tf_op jit(solution)/shard_map/step_cells/pallas_call | solution.py:482
  (1 shorter events, 0.0 us)
Async XLA Ops:
  3.4 19.7 %all-to-all-start = ((f32[4,40,128]{2,1,0:T(8,128)}), f32[4,40,128]{2,1,0:T(8,128)S(1)}, u32[]{:S(2)}, u32[]{:S(2)}) async-start(f32[4,40,128]{2,1,0:T(8,128)} %get-tuple-element.40), calls=%async_computation | async-start | bytes 163840 | tf_op jit(solution)/shard_map/all_to_all | solution.py:438
  16.1 3.3 %collective-permute-start = (f32[6,32,256]{2,1,0:T(8,128)S(1)}, f32[6,32,256]{2,1,0:T(8,128)S(1)}, u32[]{:S(2)}, u32[]{:S(2)}) collective-permute-start(f32[6,32,256]{2,1,0:T(8,128)S(1)} %get-tuple-element.36), channel_id=1, source_target_pairs={{4,8},{8,4},{12,16},{16,12},{20,24},{24,20},{28,32},{32,28},{36,40... | collective-permute-start | bytes 589832 | tf_op jit(solution)/shard_map/ppermute | solution.py:464
  16.8 3.3 %collective-permute-start.1 = (f32[6,32,256]{2,1,0:T(8,128)S(1)}, f32[6,32,256]{2,1,0:T(8,128)S(1)}, u32[]{:S(2)}, u32[]{:S(2)}) collective-permute-start(f32[6,32,256]{2,1,0:T(8,128)S(1)} %get-tuple-element.37), channel_id=1, source_target_pairs={{0,4},{4,0},{8,12},{12,8},{16,20},{20,16},{24,28},{28,24},{32,36},... | collective-permute-start | bytes 589832 | tf_op jit(solution)/shard_map/ppermute | solution.py:465

commit v6 on v5

--- a/solution.py
+++ b/solution.py
@@ -10,11 +10,13 @@
 struct_step = 1.0
 
 F32, BF16, I32 = jnp.float32, jnp.bfloat16, jnp.int32
+ORDER = (0, 2, 3, 1)
 VMEM_BYTES = 8 * 2**20
 TILE = 8
 LANES = 128
 LOADS_AT = 24
 MESSAGE_ROWS = 40
+QUARTERS = 4
 
 
 def split3(value):
@@ -24,18 +26,10 @@
     return high, middle, rest - middle
 
 
-def stack_rows(rows, total):
-    index = lax.broadcasted_iota(I32, (total, rows[0].shape[1]), 0)
-    out = jnp.zeros((total, rows[0].shape[1]), F32)
-    for at, row in enumerate(rows):
-        out = jnp.where(index == at, row, out)
-    return out
-
-
 def gather_kernel(count_in, cell_in, element_in, *refs):
     given, kept = refs[:8], refs[8:16]
-    message_out, weight_ref, third_hot, plane_hot, element_hot = refs[16:21]
-    count, cell, element, message, sems, sent = refs[21:]
+    message_out, weight_ref, third_hot, plane_hot, low_hot, pull_ref = refs[16:22]
+    count, cell, element, message, sems, sent = refs[22:]
     density, velocity, pressure, code, normal = kept[:5]
     pairs = [(cell_in, cell), (element_in, element), (count_in, count)]
     pairs += [(given[i], kept[i]) for i in (2, 3, 4, 0, 1, 5, 6, 7)]
@@ -44,7 +38,6 @@
         copy.start()
     block_x, block_y, block_z = density.shape
     rows = cell.shape[2]
-    group = element_hot.shape[0]
     col = lax.axis_index("col")
 
     copies[0].wait()
@@ -56,10 +49,16 @@
     third_hot[...] = jnp.where(third_mask, 1.0, 0.0).astype(BF16)
     plane_mask = lax.broadcasted_iota(I32, (block_x * block_y, rows), 0) == plane
     plane_hot[...] = jnp.where(plane_mask, 1.0, 0.0).astype(BF16)
-    element_mask = lax.broadcasted_iota(I32, (group, rows), 0) == element[0]
-    element_hot[...] = jnp.where(element_mask, 1.0, 0.0).astype(BF16)
+    low_mask = lax.broadcasted_iota(I32, (LANES, rows), 0) == jnp.bitwise_and(element[0], LANES - 1)
+    low_hot[...] = jnp.where(low_mask, 1.0, 0.0).astype(BF16)
     for copy in copies[2:6]:
         copy.wait()
+    line = lax.broadcasted_iota(I32, (16, rows), 0)
+    high = lax.shift_right_logical(element[0], LANES.bit_length() - 1)
+    pull = jnp.zeros((16, rows), F32)
+    for k in range(3):
+        pull = jnp.where(line == high + QUARTERS * k, normal[k, 0], pull)
+    pull_ref[...] = pull
     fraction = code[...].astype(F32) * (1.0 / 16.0)
     table = (pressure[...] * (1.0 - fraction)).reshape(block_x * block_y, block_z)
     parts = jnp.concatenate(split3(table), axis=0).astype(BF16)
@@ -83,28 +82,21 @@
         first, last = edge(x, 0), edge(x, block_y - 1)
         for j in range(message.shape[0]):
             for f in range(6):
-                row = jnp.where(col < j, last[f], first[f])
+                row = jnp.where(col < ORDER[j], last[f], first[f])
                 for h in range(2):
                     at = (2 * f + h) * block_x + x
                     message[j, at : at + 1] = row[:, h * LANES : (h + 1) * LANES]
-    for j in range(message.shape[0]):
-        message[j, LOADS_AT + 12 :] = jnp.zeros((4, LANES), F32)
     edges = slice(0, LOADS_AT)
     edge_copy = pltpu.make_async_copy(message.at[:, edges], message_out.at[:, edges], sent.at[0])
     edge_copy.start()
 
-    split = [split3(-weight * normal[k, 0]) for k in range(3)]
-    force = stack_rows([split[k][i] for i in range(3) for k in range(3)], 16).astype(BF16)
+    force = jnp.concatenate(split3(-weight * pull), axis=0).astype(BF16)
     partial = lax.dot_general(
-        force, element_hot[...], (((1,), (1,)), ((), ())), preferred_element_type=F32
-    )
-    quarters = group // LANES
-    for k in range(3):
-        total = partial[k : k + 1] + partial[3 + k : 4 + k] + partial[6 + k : 7 + k]
-        for q in range(quarters):
-            at = LOADS_AT + quarters * k + q
-            for j in range(message.shape[0]):
-                message[j, at : at + 1] = total[:, q * LANES : (q + 1) * LANES]
+        force, low_hot[...], (((1,), (1,)), ((), ())), preferred_element_type=F32
+    )
+    partial = partial[:16] + partial[16:32] + partial[32:]
+    for j in range(message.shape[0]):
+        message[j, LOADS_AT:] = partial
     loads = slice(LOADS_AT, MESSAGE_ROWS)
     load_copy = pltpu.make_async_copy(message.at[:, loads], message_out.at[:, loads], sent.at[1])
     load_copy.start()
@@ -160,8 +152,31 @@
 
 
 def inner_kernel(
-    density, velocity, pressure, code, normal, weight, third_hot, plane_hot, source, total, terms
+    density,
+    velocity,
+    pressure,
+    code,
+    normal,
+    mass,
+    removed,
+    motion,
+    weight,
+    third_hot,
+    plane_hot,
+    source,
+    total,
+    terms,
+    element,
 ):
+    element[...] = jnp.ones_like(element)
+    for q in range(QUARTERS):
+        at = slice(q * LANES, (q + 1) * LANES)
+        kept = 1.0 - removed[:, at].astype(F32)
+        for k in range(3):
+            line = slice(QUARTERS * k + q, QUARTERS * k + q + 1)
+            element[0, line] = mass[:, at]
+            element[1, line] = kept
+            element[2, line] = motion[k, :, at]
     hot = plane_hot[...]
     for k in range(3):
         source[k] = scatter(hot, third_hot, weight[...] * normal[k, 0]).reshape(density.shape)
@@ -263,18 +278,16 @@
     velocity,
     pressure,
     code,
-    normal,
-    mass,
-    removed,
-    motion,
     terms,
+    element,
     most,
     scale_ref,
     message,
     weight_ref,
     third_hot,
     plane_hot,
-    element_hot,
+    low_hot,
+    pull_ref,
     state_out,
     motion_out,
     state,
@@ -282,8 +295,6 @@
     sems,
 ):
     block_x, block_y, block_z = density.shape
-    group = mass.shape[1]
-    share = motion_out.shape[2]
     cols = message.shape[0]
     col = lax.axis_index("col")
     tiles = block_y // TILE
@@ -297,24 +308,15 @@
         at = slice(TILE, block_y - TILE)
         send(most.at[0:4, x, at], state_out.at[0:4, x, at])
 
-    keep = 1.0 - removed[...].astype(F32)
-    quarters = group // LANES
     rows = slice(LOADS_AT, MESSAGE_ROWS)
     loads = message[0, rows]
     for j in range(1, cols):
         loads = loads + message[j, rows]
-    new = []
-    for k in range(3):
-        at = quarters * k
-        load = jnp.concatenate([loads[at + q : at + q + 1] for q in range(quarters)], axis=1)
-        new.append((motion[k] + struct_step * load / mass[...]) * keep)
-    split = [split3(value) for value in new]
-    stacked = stack_rows([split[k][i] for i in range(3) for k in range(3)], 16).astype(BF16)
-    moved = jnp.dot(stacked, element_hot[...], preferred_element_type=F32)
-    work = jnp.zeros_like(weight_ref[...])
-    for k in range(3):
-        row = moved[k : k + 1] + moved[3 + k : 4 + k] + moved[6 + k : 7 + k]
-        work = work + normal[k, 0] * row
+    new = (element[2] + struct_step * loads / element[0]) * element[1]
+    parts = jnp.concatenate(split3(new), axis=0).astype(BF16)
+    moved = jnp.dot(parts, low_hot[...], preferred_element_type=F32)
+    moved = moved[:16] + moved[16:32] + moved[32:]
+    work = jnp.sum(pull_ref[...] * moved, axis=0, keepdims=True)
     found = scatter(plane_hot[...], third_hot, weight_ref[...] * work)
 
     def edge(along_y):
@@ -326,7 +328,8 @@
         out[ENE], out[SND] = terms[3, :, along_y], terms[4, :, along_y]
         return out
 
-    def arrived(j, inside):
+    def arrived(beside, inside):
+        j = sum(jnp.where(beside == c, place, 0) for place, c in enumerate(ORDER))
         got = []
         for f in range(6):
             at = 2 * f * block_x
@@ -354,9 +357,10 @@
                 state[i, x, at] = corrected(i, x, t)
             send(state.at[0:4, x, at], state_out.at[0:4, x, at])
     for k in range(3):
-        own = new[k][:, 0:share]
+        own = new[QUARTERS * k : QUARTERS * k + 1]
         for j in range(1, cols):
-            own = jnp.where(col == j, new[k][:, j * share : (j + 1) * share], own)
+            at = QUARTERS * k + j
+            own = jnp.where(col == j, new[at : at + 1], own)
         own_motion[k] = own
     send(own_motion, motion_out)
     for x in range(block_x):
@@ -415,10 +419,11 @@
             pltpu.VMEM((1, rows), F32),
             pltpu.VMEM((block_z, rows), BF16),
             pltpu.VMEM((block_x * block_y, rows), BF16),
-            pltpu.VMEM((group, rows), BF16),
+            pltpu.VMEM((LANES, rows), BF16),
+            pltpu.VMEM((16, rows), F32),
         ),
         in_specs=[pl.BlockSpec(memory_space=pl.ANY)] + [hbm] * 10,
-        out_specs=[vmem] * 8 + [hbm] + [vmem] * 4,
+        out_specs=[vmem] * 8 + [hbm] + [vmem] * 5,
         scratch_shapes=[
             pltpu.VMEM(interface_count.shape, I32),
             pltpu.VMEM(interface_cell.shape, I32),
@@ -435,7 +440,9 @@
     )
     kept, message, hots = results[:8], results[8], results[9:]
 
-    message_in = lax.all_to_all(message, "col", 0, 0)
+    message_in = lax.all_to_all(
+        message, "col", 0, 0, axis_index_groups=[list(ORDER)]
+    )
     planes = pltpu.VMEM((6, block_y, block_z), F32)
     far, near = pl.pallas_call(
         plane_kernel,
@@ -446,19 +453,20 @@
         compiler_params=pltpu.CompilerParams(vmem_limit_bytes=VMEM_BYTES),
         name="pack_planes",
     )(*in_vmem(*kept[:4]))
-    pushed, total, terms = pl.pallas_call(
+    pushed, total, terms, elements = pl.pallas_call(
         inner_kernel,
         out_shape=(
             pltpu.VMEM((3, block_x, block_y, block_z), F32),
             pltpu.VMEM((5, block_x, block_y, block_z), F32),
             pltpu.VMEM((5, block_x, block_y, block_z), F32),
+            pltpu.VMEM((3, 16, LANES), F32),
         ),
-        in_specs=[vmem] * 8,
-        out_specs=[vmem] * 3,
+        in_specs=[vmem] * 11,
+        out_specs=[vmem] * 4,
         cost_estimate=pl.CostEstimate(flops=10000000000, bytes_accessed=100000000, transcendentals=0),
         compiler_params=pltpu.CompilerParams(vmem_limit_bytes=VMEM_BYTES),
         name="inner_faces",
-    )(*in_vmem(*kept[:5], *hots[:3]))
+    )(*in_vmem(*kept, *hots[:3]))
     inner = [(i, i ^ 1) for i in range(slabs)]
     outer = [(i, i + 1 if i % 2 else i - 1) for i in range(1, slabs - 1)]
     far_in = lax.ppermute(far, "slab", outer)
@@ -485,7 +493,7 @@
             jax.ShapeDtypeStruct((5, block_x, block_y, block_z), F32),
             jax.ShapeDtypeStruct((3, 1, share), F32),
         ),
-        in_specs=[vmem] * 16,
+        in_specs=[vmem] * 14,
         out_specs=[hbm, hbm],
         scratch_shapes=[
             pltpu.VMEM((5, block_x, block_y, block_z), F32),
@@ -494,7 +502,7 @@
         ],
         compiler_params=pltpu.CompilerParams(vmem_limit_bytes=VMEM_BYTES),
         name="step_cells",
-    )(*in_vmem(*kept, terms, most, scale, message_in, *hots))
+    )(*in_vmem(*kept[:4], terms, elements, most, scale, message_in, *hots))
     return (state, new_motion)
 
 

time: 24.5 us -> 24.1 us (0.984)
  no operation moved by 1% of the time
where the time goes in v6:
time: 24.1 us; the launch traced here: 23.9 us
  starting transfers between devices  15.2 us (63%)
  Pallas kernels  4.05 us (17%)
  waiting for transfers between devices  3.26 us (14%)
  between operations  1.33 us (6%)
    all_to_all x1, starting transfers between devices, local(): lax.all_to_all(message, 'col', 0, 0, axis_index_groups=[list(ORDER)])  12.6 us
    all_to_all x1, waiting for transfers between devices, local(): lax.all_to_all(message, 'col', 0, 0, axis_index_groups=[list(ORDER)])  2.52 us
    pallas_call x1, Pallas kernels, local(): pl.pallas_call(gather_kernel, out_shape=tuple((pltpu.VMEM(array.shape, ar...  2.05 us
    ppermute x1, starting transfers between devices, local(): near_in = lax.ppermute(near, 'slab', inner)  1.92 us
    pallas_call x1, Pallas kernels, local(): pl.pallas_call(step_kernel, out_shape=(jax.ShapeDtypeStruct((5, block_x,...  1.06 us
    ppermute x1, waiting for transfers between devices, local(): near_in = lax.ppermute(near, 'slab', inner)  0.73 us
    ppermute x1, starting transfers between devices, local(): far_in = lax.ppermute(far, 'slab', outer)  0.67 us
    pallas_call x1, Pallas kernels, local(): pl.pallas_call(inner_kernel, out_shape=(pltpu.VMEM((3, block_x, block_y,...  0.66 us
  transfers between devices with their start and end apart: 3, of which 2 were waited for; matrix products, arithmetic and copies ran while one was open for 0% of the time, Pallas kernels for 4%

profile of v6, /device:TPU:16, one launch (start us, length us, event | category | flops | bytes accessed | tf_op | source)
XLA Modules:
  0.0 23.9 jit_solution(1651909744762345755)
XLA Ops:
  1.3 2.1 %gather_rows.1 = (f32[2,32,256]{2,1,0:T(8,128)S(1)}, f32[3,2,32,256]{3,2,1,0:T(8,128)S(1)}, f32[2,32,256]{2,1,0:T(8,128)S(1)}, s32[2,32,256]{2,1,0:T(8,128)S(1)}...) custom-call(s32[1,1]{1,0:T(1,128)S(6)} %copy.13.count_in, ...), custom_call_target="tpu_custom_call" | custom-call | tf_op jit(solution)/shard_map/gather_rows/pallas_call | solution.py:414
  3.3 12.6 %all-to-all-start = ((f32[4,40,128]{2,1,0:T(8,128)}), f32[4,40,128]{2,1,0:T(8,128)S(1)}, u32[]{:S(2)}, u32[]{:S(2)}) async-start(f32[4,40,128]{2,1,0:T(8,128)} %get-tuple-element.43), calls=%async_computation | async-start | bytes 163840 | tf_op jit(solution)/shard_map/all_to_all | solution.py:443
  16.0 0.7 %collective-permute-start = (f32[6,32,256]{2,1,0:T(8,128)S(1)}, f32[6,32,256]{2,1,0:T(8,128)S(1)}, u32[]{:S(2)}, u32[]{:S(2)}) collective-permute-start(f32[6,32,256]{2,1,0:T(8,128)S(1)} %get-tuple-element.39), channel_id=1, source_target_pairs={{4,8},{8,4},{12,16},{16,12},{20,24},{24,20},{28,32},{32,28},{36,40... | collective-permute-start | bytes 589832 | tf_op jit(solution)/shard_map/ppermute | solution.py:472
  16.7 1.9 %collective-permute-start.1 = (f32[6,32,256]{2,1,0:T(8,128)S(1)}, f32[6,32,256]{2,1,0:T(8,128)S(1)}, u32[]{:S(2)}, u32[]{:S(2)}) collective-permute-start(f32[6,32,256]{2,1,0:T(8,128)S(1)} %get-tuple-element.40), channel_id=1, source_target_pairs={{0,4},{4,0},{8,12},{12,8},{16,20},{20,16},{24,28},{28,24},{32,36},... | collective-permute-start | bytes 589832 | tf_op jit(solution)/shard_map/ppermute | solution.py:473
  18.6 0.7 %inner_faces.1 = (f32[3,2,32,256]{3,2,1,0:T(8,128)S(1)}, f32[5,2,32,256]{3,2,1,0:T(8,128)S(1)}, f32[5,2,32,256]{3,2,1,0:T(8,128)S(1)}, f32[3,16,128]{2,1,0:T(8,128)S(1)}) custom-call(f32[2,32,256]{2,1,0:T(8,128)S(1)} %get-tuple-element.24.density, f32[3,2,32,256]{3,2,1,0:T(8,128)S(1)} %get-tuple-element.25.velocity, ...), custom_call_target="tpu_custom_call" | custom-call | flops 10000000000 | bytes 100000000 | tf_op jit(solution)/shard_map/inner_faces/pallas_call | solution.py:456
  19.3 0.0 collective-permute-done.far_ref
  19.3 0.7 %collective-permute-done.1.near_ref = f32[6,32,256]{2,1,0:T(8,128)S(1)} collective-permute-done((f32[6,32,256]{2,1,0:T(8,128)S(1)}, f32[6,32,256]{2,1,0:T(8,128)S(1)}, u32[]{:S(2)}, u32[]{:S(2)}) %collective-permute-start.1) | collective-permute-done | bytes 196640 | tf_op jit(solution)/shard_map/ppermute | solution.py:473
  20.0 0.2 %outer_faces.1 = (f32[5,2,32,256]{3,2,1,0:T(8,128)S(1)}, f32[2,32,256]{2,1,0:T(8,128)S(1)}) custom-call(f32[2,32,256]{2,1,0:T(8,128)S(1)} %get-tuple-element.24.density, f32[3,2,32,256]{3,2,1,0:T(8,128)S(1)} %get-tuple-element.25.velocity, f32[2,32,256]{2,1,0:T(8,128)S(1)} %get-tuple-element.26.pressure, s32[2,32,256]{2,1,0:T(8,128)S(1)} %get-tuple-element.27.code, ...), custom_call_target="tpu_custom_call" | custom-call | flops 1638400 | bytes 1048576 | tf_op jit(solution)/shard_map/outer_faces/pallas_call | solution.py:476
  20.3 2.5 %all-to-all-done.message = f32[4,40,128]{2,1,0:T(8,128)S(1)} async-done(((f32[4,40,128]{2,1,0:T(8,128)}), f32[4,40,128]{2,1,0:T(8,128)S(1)}, u32[]{:S(2)}, u32[]{:S(2)}) %all-to-all-start) | async-done | bytes 81952 | tf_op jit(solution)/shard_map/all_to_all | solution.py:443
  22.8 1.1 %step_cells.1 = (f32[5,2,32,256]{3,2,1,0:T(8,128)}, f32[3,1,128]{2,1,0:T(1,128)}) custom-call(f32[2,32,256]{2,1,0:T(8,128)S(1)} %get-tuple-element.24.density, f32[3,2,32,256]{3,2,1,0:T(8,128)S(1)} %get-tuple-element.25.velocity, f32[2,32,256]{2,1,0:T(8,128)S(1)} %get-tuple-element.26.pressure, s32[2,32,256]{2,1,0:T(8,128)S(1)} %get-tuple-element.27.code, ...), custom_call_target="tpu_custom_call" | custom-call | tf_op jit(solution)/shard_map/step_cells/pallas_call | solution.py:490
  (1 shorter events, 0.0 us)
Async XLA Ops:
  3.3 19.5 %all-to-all-start = ((f32[4,40,128]{2,1,0:T(8,128)}), f32[4,40,128]{2,1,0:T(8,128)S(1)}, u32[]{:S(2)}, u32[]{:S(2)}) async-start(f32[4,40,128]{2,1,0:T(8,128)} %get-tuple-element.43), calls=%async_computation | async-start | bytes 163840 | tf_op jit(solution)/shard_map/all_to_all | solution.py:443
  16.0 3.3 %collective-permute-start = (f32[6,32,256]{2,1,0:T(8,128)S(1)}, f32[6,32,256]{2,1,0:T(8,128)S(1)}, u32[]{:S(2)}, u32[]{:S(2)}) collective-permute-start(f32[6,32,256]{2,1,0:T(8,128)S(1)} %get-tuple-element.39), channel_id=1, source_target_pairs={{4,8},{8,4},{12,16},{16,12},{20,24},{24,20},{28,32},{32,28},{36,40... | collective-permute-start | bytes 589832 | tf_op jit(solution)/shard_map/ppermute | solution.py:472
  16.7 3.3 %collective-permute-start.1 = (f32[6,32,256]{2,1,0:T(8,128)S(1)}, f32[6,32,256]{2,1,0:T(8,128)S(1)}, u32[]{:S(2)}, u32[]{:S(2)}) collective-permute-start(f32[6,32,256]{2,1,0:T(8,128)S(1)} %get-tuple-element.40), channel_id=1, source_target_pairs={{0,4},{4,0},{8,12},{12,8},{16,20},{20,16},{24,28},{28,24},{32,36},... | collective-permute-start | bytes 589832 | tf_op jit(solution)/shard_map/ppermute | solution.py:473

commit v7 on v6

--- a/solution.py
+++ b/solution.py
@@ -174,7 +174,7 @@
         kept = 1.0 - removed[:, at].astype(F32)
         for k in range(3):
             line = slice(QUARTERS * k + q, QUARTERS * k + q + 1)
-            element[0, line] = mass[:, at]
+            element[0, line] = struct_step / mass[:, at]
             element[1, line] = kept
             element[2, line] = motion[k, :, at]
     hot = plane_hot[...]
@@ -304,15 +304,14 @@
         copies.append(pltpu.make_async_copy(source, target, sems.at[len(copies)]))
         copies[-1].start()
 
-    for x in range(block_x):
-        at = slice(TILE, block_y - TILE)
-        send(most.at[0:4, x, at], state_out.at[0:4, x, at])
+    at = slice(TILE, block_y - TILE)
+    send(most.at[0:4, :, at], state_out.at[0:4, :, at])
 
     rows = slice(LOADS_AT, MESSAGE_ROWS)
     loads = message[0, rows]
     for j in range(1, cols):
         loads = loads + message[j, rows]
-    new = (element[2] + struct_step * loads / element[0]) * element[1]
+    new = (element[2] + loads * element[0]) * element[1]
     parts = jnp.concatenate(split3(new), axis=0).astype(BF16)
     moved = jnp.dot(parts, low_hot[...], preferred_element_type=F32)
     moved = moved[:16] + moved[16:32] + moved[32:]
@@ -350,12 +349,12 @@
             value = value - jnp.where(row == TILE - 1, scale_ref[x, at] * top[i][x : x + 1], 0.0)
         return value
 
-    for x in range(block_x):
-        for t in (0, tiles - 1):
-            at = slice(t * TILE, (t + 1) * TILE)
+    for t in (0, tiles - 1):
+        at = slice(t * TILE, (t + 1) * TILE)
+        for x in range(block_x):
             for i in range(4):
                 state[i, x, at] = corrected(i, x, t)
-            send(state.at[0:4, x, at], state_out.at[0:4, x, at])
+        send(state.at[0:4, :, at], state_out.at[0:4, :, at])
     for k in range(3):
         own = new[QUARTERS * k : QUARTERS * k + 1]
         for j in range(1, cols):
@@ -498,7 +497,7 @@
         scratch_shapes=[
             pltpu.VMEM((5, block_x, block_y, block_z), F32),
             pltpu.VMEM((3, 1, share), F32),
-            pltpu.SemaphoreType.DMA((3 * block_x + 2,)),
+            pltpu.SemaphoreType.DMA((5,)),
         ],
         compiler_params=pltpu.CompilerParams(vmem_limit_bytes=VMEM_BYTES),
         name="step_cells",

time: 24.1 us -> 24.1 us (level)
  no operation moved by 1% of the time
where the time goes in v7:
time: 24.1 us; the launch traced here: 23.8 us
  starting transfers between devices  15.2 us (63%)
  Pallas kernels  4.01 us (17%)
  waiting for transfers between devices  3.26 us (14%)
  between operations  1.33 us (6%)
    all_to_all x1, starting transfers between devices, local(): lax.all_to_all(message, 'col', 0, 0, axis_index_groups=[list(ORDER)])  12.6 us
    all_to_all x1, waiting for transfers between devices, local(): lax.all_to_all(message, 'col', 0, 0, axis_index_groups=[list(ORDER)])  2.52 us
    pallas_call x1, Pallas kernels, local(): pl.pallas_call(gather_kernel, out_shape=tuple((pltpu.VMEM(array.shape, ar...  2.05 us
    ppermute x1, starting transfers between devices, local(): near_in = lax.ppermute(near, 'slab', inner)  1.92 us
    pallas_call x1, Pallas kernels, local(): pl.pallas_call(step_kernel, out_shape=(jax.ShapeDtypeStruct((5, block_x,...  1.02 us
    ppermute x1, waiting for transfers between devices, local(): near_in = lax.ppermute(near, 'slab', inner)  0.73 us
    ppermute x1, starting transfers between devices, local(): far_in = lax.ppermute(far, 'slab', outer)  0.67 us
    pallas_call x1, Pallas kernels, local(): pl.pallas_call(inner_kernel, out_shape=(pltpu.VMEM((3, block_x, block_y,...  0.66 us
  transfers between devices with their start and end apart: 3, of which 2 were waited for; matrix products, arithmetic and copies ran while one was open for 0% of the time, Pallas kernels for 4%

profile of v7, /device:TPU:16, one launch (start us, length us, event | category | flops | bytes accessed | tf_op | source)
XLA Modules:
  0.0 23.8 jit_solution(17373139262002117153)
XLA Ops:
  1.3 2.1 %gather_rows.1 = (f32[2,32,256]{2,1,0:T(8,128)S(1)}, f32[3,2,32,256]{3,2,1,0:T(8,128)S(1)}, f32[2,32,256]{2,1,0:T(8,128)S(1)}, s32[2,32,256]{2,1,0:T(8,128)S(1)}...) custom-call(s32[1,1]{1,0:T(1,128)S(6)} %copy.13.count_in, ...), custom_call_target="tpu_custom_call" | custom-call | tf_op jit(solution)/shard_map/gather_rows/pallas_call | solution.py:413
  3.3 12.6 %all-to-all-start = ((f32[4,40,128]{2,1,0:T(8,128)}), f32[4,40,128]{2,1,0:T(8,128)S(1)}, u32[]{:S(2)}, u32[]{:S(2)}) async-start(f32[4,40,128]{2,1,0:T(8,128)} %get-tuple-element.43), calls=%async_computation | async-start | bytes 163840 | tf_op jit(solution)/shard_map/all_to_all | solution.py:442
  16.0 0.7 %collective-permute-start = (f32[6,32,256]{2,1,0:T(8,128)S(1)}, f32[6,32,256]{2,1,0:T(8,128)S(1)}, u32[]{:S(2)}, u32[]{:S(2)}) collective-permute-start(f32[6,32,256]{2,1,0:T(8,128)S(1)} %get-tuple-element.39), channel_id=1, source_target_pairs={{4,8},{8,4},{12,16},{16,12},{20,24},{24,20},{28,32},{32,28},{36,40... | collective-permute-start | bytes 589832 | tf_op jit(solution)/shard_map/ppermute | solution.py:471
  16.7 1.9 %collective-permute-start.1 = (f32[6,32,256]{2,1,0:T(8,128)S(1)}, f32[6,32,256]{2,1,0:T(8,128)S(1)}, u32[]{:S(2)}, u32[]{:S(2)}) collective-permute-start(f32[6,32,256]{2,1,0:T(8,128)S(1)} %get-tuple-element.40), channel_id=1, source_target_pairs={{0,4},{4,0},{8,12},{12,8},{16,20},{20,16},{24,28},{28,24},{32,36},... | collective-permute-start | bytes 589832 | tf_op jit(solution)/shard_map/ppermute | solution.py:472
  18.6 0.7 %inner_faces.1 = (f32[3,2,32,256]{3,2,1,0:T(8,128)S(1)}, f32[5,2,32,256]{3,2,1,0:T(8,128)S(1)}, f32[5,2,32,256]{3,2,1,0:T(8,128)S(1)}, f32[3,16,128]{2,1,0:T(8,128)S(1)}) custom-call(f32[2,32,256]{2,1,0:T(8,128)S(1)} %get-tuple-element.24.density, f32[3,2,32,256]{3,2,1,0:T(8,128)S(1)} %get-tuple-element.25.velocity, ...), custom_call_target="tpu_custom_call" | custom-call | flops 10000000000 | bytes 100000000 | tf_op jit(solution)/shard_map/inner_faces/pallas_call | solution.py:455
  19.3 0.0 collective-permute-done.far_ref
  19.3 0.7 %collective-permute-done.1.near_ref = f32[6,32,256]{2,1,0:T(8,128)S(1)} collective-permute-done((f32[6,32,256]{2,1,0:T(8,128)S(1)}, f32[6,32,256]{2,1,0:T(8,128)S(1)}, u32[]{:S(2)}, u32[]{:S(2)}) %collective-permute-start.1) | collective-permute-done | bytes 196640 | tf_op jit(solution)/shard_map/ppermute | solution.py:472
  20.0 0.2 %outer_faces.1 = (f32[5,2,32,256]{3,2,1,0:T(8,128)S(1)}, f32[2,32,256]{2,1,0:T(8,128)S(1)}) custom-call(f32[2,32,256]{2,1,0:T(8,128)S(1)} %get-tuple-element.24.density, f32[3,2,32,256]{3,2,1,0:T(8,128)S(1)} %get-tuple-element.25.velocity, f32[2,32,256]{2,1,0:T(8,128)S(1)} %get-tuple-element.26.pressure, s32[2,32,256]{2,1,0:T(8,128)S(1)} %get-tuple-element.27.code, ...), custom_call_target="tpu_custom_call" | custom-call | flops 1638400 | bytes 1048576 | tf_op jit(solution)/shard_map/outer_faces/pallas_call | solution.py:475
  20.3 2.5 %all-to-all-done.message = f32[4,40,128]{2,1,0:T(8,128)S(1)} async-done(((f32[4,40,128]{2,1,0:T(8,128)}), f32[4,40,128]{2,1,0:T(8,128)S(1)}, u32[]{:S(2)}, u32[]{:S(2)}) %all-to-all-start) | async-done | bytes 81952 | tf_op jit(solution)/shard_map/all_to_all | solution.py:442
  22.8 1.0 %step_cells.1 = (f32[5,2,32,256]{3,2,1,0:T(8,128)}, f32[3,1,128]{2,1,0:T(1,128)}) custom-call(f32[2,32,256]{2,1,0:T(8,128)S(1)} %get-tuple-element.24.density, f32[3,2,32,256]{3,2,1,0:T(8,128)S(1)} %get-tuple-element.25.velocity, f32[2,32,256]{2,1,0:T(8,128)S(1)} %get-tuple-element.26.pressure, s32[2,32,256]{2,1,0:T(8,128)S(1)} %get-tuple-element.27.code, ...), custom_call_target="tpu_custom_call" | custom-call | tf_op jit(solution)/shard_map/step_cells/pallas_call | solution.py:489
  (1 shorter events, 0.0 us)
Async XLA Ops:
  3.3 19.5 %all-to-all-start = ((f32[4,40,128]{2,1,0:T(8,128)}), f32[4,40,128]{2,1,0:T(8,128)S(1)}, u32[]{:S(2)}, u32[]{:S(2)}) async-start(f32[4,40,128]{2,1,0:T(8,128)} %get-tuple-element.43), calls=%async_computation | async-start | bytes 163840 | tf_op jit(solution)/shard_map/all_to_all | solution.py:442
  16.0 3.3 %collective-permute-start = (f32[6,32,256]{2,1,0:T(8,128)S(1)}, f32[6,32,256]{2,1,0:T(8,128)S(1)}, u32[]{:S(2)}, u32[]{:S(2)}) collective-permute-start(f32[6,32,256]{2,1,0:T(8,128)S(1)} %get-tuple-element.39), channel_id=1, source_target_pairs={{4,8},{8,4},{12,16},{16,12},{20,24},{24,20},{28,32},{32,28},{36,40... | collective-permute-start | bytes 589832 | tf_op jit(solution)/shard_map/ppermute | solution.py:471
  16.7 3.3 %collective-permute-start.1 = (f32[6,32,256]{2,1,0:T(8,128)S(1)}, f32[6,32,256]{2,1,0:T(8,128)S(1)}, u32[]{:S(2)}, u32[]{:S(2)}) collective-permute-start(f32[6,32,256]{2,1,0:T(8,128)S(1)} %get-tuple-element.40), channel_id=1, source_target_pairs={{0,4},{4,0},{8,12},{12,8},{16,20},{20,16},{24,28},{28,24},{32,36},... | collective-permute-start | bytes 589832 | tf_op jit(solution)/shard_map/ppermute | solution.py:472

commit v8 on v7

--- a/solution.py
+++ b/solution.py
@@ -27,12 +27,12 @@
 
 
 def gather_kernel(count_in, cell_in, element_in, *refs):
-    given, kept = refs[:8], refs[8:16]
-    message_out, weight_ref, third_hot, plane_hot, low_hot, pull_ref = refs[16:22]
-    count, cell, element, message, sems, sent = refs[22:]
+    given, kept = refs[:5], refs[5:10]
+    message_out, weight_ref, third_hot, plane_hot, low_hot, pull_ref = refs[10:16]
+    count, cell, element, message, sems, sent = refs[16:]
     density, velocity, pressure, code, normal = kept[:5]
     pairs = [(cell_in, cell), (element_in, element), (count_in, count)]
-    pairs += [(given[i], kept[i]) for i in (2, 3, 4, 0, 1, 5, 6, 7)]
+    pairs += [(given[i], kept[i]) for i in (2, 3, 4, 0, 1)]
     copies = [pltpu.make_async_copy(a, b, sems.at[i]) for i, (a, b) in enumerate(pairs)]
     for copy in copies:
         copy.start()
@@ -157,9 +157,9 @@
     pressure,
     code,
     normal,
-    mass,
-    removed,
-    motion,
+    mass_in,
+    removed_in,
+    motion_in,
     weight,
     third_hot,
     plane_hot,
@@ -167,16 +167,15 @@
     total,
     terms,
     element,
+    mass,
+    removed,
+    motion,
+    sems,
 ):
-    element[...] = jnp.ones_like(element)
-    for q in range(QUARTERS):
-        at = slice(q * LANES, (q + 1) * LANES)
-        kept = 1.0 - removed[:, at].astype(F32)
-        for k in range(3):
-            line = slice(QUARTERS * k + q, QUARTERS * k + q + 1)
-            element[0, line] = struct_step / mass[:, at]
-            element[1, line] = kept
-            element[2, line] = motion[k, :, at]
+    pairs = ((mass_in, mass), (removed_in, removed), (motion_in, motion))
+    copies = [pltpu.make_async_copy(a, b, sems.at[i]) for i, (a, b) in enumerate(pairs)]
+    for copy in copies:
+        copy.start()
     hot = plane_hot[...]
     for k in range(3):
         source[k] = scatter(hot, third_hot, weight[...] * normal[k, 0]).reshape(density.shape)
@@ -239,6 +238,17 @@
                 first = jnp.zeros_like(turned[i]) if before is None else before[i]
                 total[i, x, at] += upper[i] - jnp.where(row == 0, first, turned[i])
             before = turned
+    for copy in copies:
+        copy.wait()
+    element[...] = jnp.ones_like(element)
+    for q in range(QUARTERS):
+        at = slice(q * LANES, (q + 1) * LANES)
+        kept = 1.0 - removed[:, at].astype(F32)
+        for k in range(3):
+            line = slice(QUARTERS * k + q, QUARTERS * k + q + 1)
+            element[0, line] = struct_step / mass[:, at]
+            element[1, line] = kept
+            element[2, line] = motion[k, :, at]
 
 
 def other(prims, fraction):
@@ -406,9 +416,6 @@
         pressure,
         fraction_code,
         wall_normal,
-        element_mass,
-        element_removed,
-        element_velocity,
     )
     results = pl.pallas_call(
         gather_kernel,
@@ -421,14 +428,14 @@
             pltpu.VMEM((LANES, rows), BF16),
             pltpu.VMEM((16, rows), F32),
         ),
-        in_specs=[pl.BlockSpec(memory_space=pl.ANY)] + [hbm] * 10,
-        out_specs=[vmem] * 8 + [hbm] + [vmem] * 5,
+        in_specs=[pl.BlockSpec(memory_space=pl.ANY)] + [hbm] * 7,
+        out_specs=[vmem] * 5 + [hbm] + [vmem] * 5,
         scratch_shapes=[
             pltpu.VMEM(interface_count.shape, I32),
             pltpu.VMEM(interface_cell.shape, I32),
             pltpu.VMEM(interface_element.shape, I32),
             pltpu.VMEM((cols, MESSAGE_ROWS, LANES), F32),
-            pltpu.SemaphoreType.DMA((11,)),
+            pltpu.SemaphoreType.DMA((8,)),
             pltpu.SemaphoreType.DMA((2,)),
         ],
         compiler_params=pltpu.CompilerParams(vmem_limit_bytes=VMEM_BYTES),
@@ -437,7 +444,7 @@
         interface_count,
         *in_hbm(interface_cell, interface_element, *given),
     )
-    kept, message, hots = results[:8], results[8], results[9:]
+    kept, message, hots = results[:5], results[5], results[6:]
 
     message_in = lax.all_to_all(
         message, "col", 0, 0, axis_index_groups=[list(ORDER)]
@@ -460,12 +467,22 @@
             pltpu.VMEM((5, block_x, block_y, block_z), F32),
             pltpu.VMEM((3, 16, LANES), F32),
         ),
-        in_specs=[vmem] * 11,
+        in_specs=[vmem] * 5 + [hbm] * 3 + [vmem] * 3,
         out_specs=[vmem] * 4,
+        scratch_shapes=[
+            pltpu.VMEM(element_mass.shape, F32),
+            pltpu.VMEM(element_removed.shape, I32),
+            pltpu.VMEM(element_velocity.shape, F32),
+            pltpu.SemaphoreType.DMA((3,)),
+        ],
         cost_estimate=pl.CostEstimate(flops=10000000000, bytes_accessed=100000000, transcendentals=0),
         compiler_params=pltpu.CompilerParams(vmem_limit_bytes=VMEM_BYTES),
         name="inner_faces",
-    )(*in_vmem(*kept, *hots[:3]))
+    )(
+        *in_vmem(*kept),
+        *in_hbm(element_mass, element_removed, element_velocity),
+        *in_vmem(*hots[:3]),
+    )
     inner = [(i, i ^ 1) for i in range(slabs)]
     outer = [(i, i + 1 if i % 2 else i - 1) for i in range(1, slabs - 1)]
     far_in = lax.ppermute(far, "slab", outer)

time: 24.1 us -> 24.1 us (level)
  waiting for transfers between devices: 3.26 us -> 2.6 us
  Pallas kernels: 4.01 us -> 4.64 us
    ppermute x1, waiting for transfers between devices: 0.73 us -> 0.07 us  [local(): near_in = lax.ppermute(near, 'slab', inner)]
    pallas_call x1, Pallas kernels: 0.66 us -> 1.31 us  [local(): pl.pallas_call(inner_kernel, out_shape=(pltpu.VMEM((3, block_x, block_y,...]
  transfers between devices with their start and end apart: 3 -> 3, of which waited for: 2 -> 2; matrix products, arithmetic and copies ran while one was open for 0% -> 0% of each run, Pallas kernels for 4% -> 7%
where the time goes in v8:
time: 24.1 us; the launch traced here: 23.8 us
  starting transfers between devices  15.2 us (63%)
  Pallas kernels  4.64 us (19%)
  waiting for transfers between devices  2.6 us (11%)
  between operations  1.33 us (6%)
    all_to_all x1, starting transfers between devices, local(): lax.all_to_all(message, 'col', 0, 0, axis_index_groups=[list(ORDER)])  12.6 us
    all_to_all x1, waiting for transfers between devices, local(): lax.all_to_all(message, 'col', 0, 0, axis_index_groups=[list(ORDER)])  2.52 us
    pallas_call x1, Pallas kernels, local(): pl.pallas_call(gather_kernel, out_shape=tuple((pltpu.VMEM(array.shape, ar...  2.02 us
    ppermute x1, starting transfers between devices, local(): near_in = lax.ppermute(near, 'slab', inner)  1.92 us
    pallas_call x1, Pallas kernels, local(): pl.pallas_call(inner_kernel, out_shape=(pltpu.VMEM((3, block_x, block_y,...  1.31 us
    pallas_call x1, Pallas kernels, local(): pl.pallas_call(step_kernel, out_shape=(jax.ShapeDtypeStruct((5, block_x,...  1.02 us
    ppermute x1, starting transfers between devices, local(): far_in = lax.ppermute(far, 'slab', outer)  0.67 us
  transfers between devices with their start and end apart: 3, of which 2 were waited for; matrix products, arithmetic and copies ran while one was open for 0% of the time, Pallas kernels for 7%

profile of v8, /device:TPU:16, one launch (start us, length us, event | category | flops | bytes accessed | tf_op | source)
XLA Modules:
  0.0 23.8 jit_solution(2051826318606808474)
XLA Ops:
  1.3 2.0 %gather_rows.1 = (f32[2,32,256]{2,1,0:T(8,128)S(1)}, f32[3,2,32,256]{3,2,1,0:T(8,128)S(1)}, f32[2,32,256]{2,1,0:T(8,128)S(1)}, s32[2,32,256]{2,1,0:T(8,128)S(1)}...) custom-call(s32[1,1]{1,0:T(1,128)S(6)} %copy.13.count_in, ...), custom_call_target="tpu_custom_call" | custom-call | tf_op jit(solution)/shard_map/gather_rows/pallas_call | solution.py:420
  3.3 12.6 %all-to-all-start = ((f32[4,40,128]{2,1,0:T(8,128)}), f32[4,40,128]{2,1,0:T(8,128)S(1)}, u32[]{:S(2)}, u32[]{:S(2)}) async-start(f32[4,40,128]{2,1,0:T(8,128)} %get-tuple-element.37), calls=%async_computation | async-start | bytes 163840 | tf_op jit(solution)/shard_map/all_to_all | solution.py:449
  16.0 0.7 %collective-permute-start = (f32[6,32,256]{2,1,0:T(8,128)S(1)}, f32[6,32,256]{2,1,0:T(8,128)S(1)}, u32[]{:S(2)}, u32[]{:S(2)}) collective-permute-start(f32[6,32,256]{2,1,0:T(8,128)S(1)} %get-tuple-element.33), channel_id=1, source_target_pairs={{4,8},{8,4},{12,16},{16,12},{20,24},{24,20},{28,32},{32,28},{36,40... | collective-permute-start | bytes 589832 | tf_op jit(solution)/shard_map/ppermute | solution.py:488
  16.6 1.9 %collective-permute-start.1 = (f32[6,32,256]{2,1,0:T(8,128)S(1)}, f32[6,32,256]{2,1,0:T(8,128)S(1)}, u32[]{:S(2)}, u32[]{:S(2)}) collective-permute-start(f32[6,32,256]{2,1,0:T(8,128)S(1)} %get-tuple-element.34), channel_id=1, source_target_pairs={{0,4},{4,0},{8,12},{12,8},{16,20},{20,16},{24,28},{28,24},{32,36},... | collective-permute-start | bytes 589832 | tf_op jit(solution)/shard_map/ppermute | solution.py:489
  18.6 1.3 %inner_faces.1 = (f32[3,2,32,256]{3,2,1,0:T(8,128)S(1)}, f32[5,2,32,256]{3,2,1,0:T(8,128)S(1)}, f32[5,2,32,256]{3,2,1,0:T(8,128)S(1)}, f32[3,16,128]{2,1,0:T(8,128)S(1)}) custom-call(f32[2,32,256]{2,1,0:T(8,128)S(1)} %get-tuple-element.21.density, f32[3,2,32,256]{3,2,1,0:T(8,128)S(1)} %get-tuple-element.22.velocity, ...), custom_call_target="tpu_custom_call" | custom-call | flops 10000000000 | bytes 100000000 | tf_op jit(solution)/shard_map/inner_faces/pallas_call | solution.py:462
  19.9 0.0 collective-permute-done.far_ref
  19.9 0.1 collective-permute-done.1.near_ref
  20.0 0.2 %outer_faces.1 = (f32[5,2,32,256]{3,2,1,0:T(8,128)S(1)}, f32[2,32,256]{2,1,0:T(8,128)S(1)}) custom-call(f32[2,32,256]{2,1,0:T(8,128)S(1)} %get-tuple-element.21.density, f32[3,2,32,256]{3,2,1,0:T(8,128)S(1)} %get-tuple-element.22.velocity, f32[2,32,256]{2,1,0:T(8,128)S(1)} %get-tuple-element.23.pressure, s32[2,32,256]{2,1,0:T(8,128)S(1)} %get-tuple-element.24.code, ...), custom_call_target="tpu_custom_call" | custom-call | flops 1638400 | bytes 1048576 | tf_op jit(solution)/shard_map/outer_faces/pallas_call | solution.py:492
  20.2 2.5 %all-to-all-done.message = f32[4,40,128]{2,1,0:T(8,128)S(1)} async-done(((f32[4,40,128]{2,1,0:T(8,128)}), f32[4,40,128]{2,1,0:T(8,128)S(1)}, u32[]{:S(2)}, u32[]{:S(2)}) %all-to-all-start) | async-done | bytes 81952 | tf_op jit(solution)/shard_map/all_to_all | solution.py:449
  22.8 1.0 %step_cells.1 = (f32[5,2,32,256]{3,2,1,0:T(8,128)}, f32[3,1,128]{2,1,0:T(1,128)}) custom-call(f32[2,32,256]{2,1,0:T(8,128)S(1)} %get-tuple-element.21.density, f32[3,2,32,256]{3,2,1,0:T(8,128)S(1)} %get-tuple-element.22.velocity, f32[2,32,256]{2,1,0:T(8,128)S(1)} %get-tuple-element.23.pressure, s32[2,32,256]{2,1,0:T(8,128)S(1)} %get-tuple-element.24.code, ...), custom_call_target="tpu_custom_call" | custom-call | tf_op jit(solution)/shard_map/step_cells/pallas_call | solution.py:506
  (1 shorter events, 0.0 us)
Async XLA Ops:
  3.3 19.4 %all-to-all-start = ((f32[4,40,128]{2,1,0:T(8,128)}), f32[4,40,128]{2,1,0:T(8,128)S(1)}, u32[]{:S(2)}, u32[]{:S(2)}) async-start(f32[4,40,128]{2,1,0:T(8,128)} %get-tuple-element.37), calls=%async_computation | async-start | bytes 163840 | tf_op jit(solution)/shard_map/all_to_all | solution.py:449
  16.0 3.9 %collective-permute-start = (f32[6,32,256]{2,1,0:T(8,128)S(1)}, f32[6,32,256]{2,1,0:T(8,128)S(1)}, u32[]{:S(2)}, u32[]{:S(2)}) collective-permute-start(f32[6,32,256]{2,1,0:T(8,128)S(1)} %get-tuple-element.33), channel_id=1, source_target_pairs={{4,8},{8,4},{12,16},{16,12},{20,24},{24,20},{28,32},{32,28},{36,40... | collective-permute-start | bytes 589832 | tf_op jit(solution)/shard_map/ppermute | solution.py:488
  16.6 3.3 %collective-permute-start.1 = (f32[6,32,256]{2,1,0:T(8,128)S(1)}, f32[6,32,256]{2,1,0:T(8,128)S(1)}, u32[]{:S(2)}, u32[]{:S(2)}) collective-permute-start(f32[6,32,256]{2,1,0:T(8,128)S(1)} %get-tuple-element.34), channel_id=1, source_target_pairs={{0,4},{4,0},{8,12},{12,8},{16,20},{20,16},{24,28},{28,24},{32,36},... | collective-permute-start | bytes 589832 | tf_op jit(solution)/shard_map/ppermute | solution.py:489
